TPU v7x, 512 devices: a whole 4x8x8 slice. The times are simulated.
512 devices in a mesh: space: 32 (over z, x), vel: 16 (over y, core).
Axes of the slice: x: 4, y: 8, z: 8, core: 2. Of those that a mesh axis runs over, the one named last changes fastest.
Arguments:
- dist: bfloat16 [512, 64, 4096], P('space', None, 'vel'), may hold values from -6 to 6
- send_faces: int32 [32, 2, 16], P('space'), may hold values from 0 to 95
- send_count: int32 [32, 2], P('space'), may hold values from 1 to 16, as said below
- source_face: int32 [512, 6], P('space'), may hold values from 0 to 127, as said below
- subface: int32 [512, 6], P('space'), may hold values from 0 to 4
- alpha: float32 [4, 4096], replicated, may hold values from -1 to 1
- beta: float32 [5, 4096], replicated, may hold values from -1 to 1
Outputs:
- relaxed: bfloat16 [512, 64, 4096], P('space', None, 'vel')
Inputs may be any that keep to these rules, and one draw needn't show every extreme that they name: `source_face`: for each face of a block: below 96 a local face of the same block; from 96 the 16 slots of the previous block's block toward the next one, then the 16 slots of the next block's block toward the previous one. Every slot of these two blocks is read by exactly one face of the block. `send_count`: for each direction some block's padded trace block is full. `send_faces`: local face numbers, element times 6 plus face.
All inputs are finite; a program needn't handle non-finite values.
Results may differ from a plain program's by a relative error of at most 0.0057.
Values may be sent and summed in bfloat16 or wider, within the bound.
No kernel may reach another device: no remote copies, remote signals or barrier semaphores. Data moves between devices by JAX's collectives and lax.ppermute only.
A program may use at most 64 MiB of HBM per device.

v0:
```python
import jax
import jax.numpy as jnp
import numpy as np
from jax import lax
from jax.sharding import PartitionSpec as P

VSIDE = 16
VEL = 4096


courant = 0.1
lift_weight = 6.0
relax_step = 0.5
highest = lax.Precision.HIGHEST


def passed_along(block, axis, distance):
    devices = range(lax.axis_size(axis))
    route = [((i - distance) % len(devices), i) for i in devices]
    return lax.ppermute(block, axis, route)


def shortened(array):

    def short(part):
        return part.astype(jnp.bfloat16) if part.dtype == jnp.float32 else part

    return jax.tree.map(short, array)


def lobatto_points():
    return np.array([-1.0, -1.0 / np.sqrt(5.0), 1.0 / np.sqrt(5.0), 1.0])


def lagrange_table(targets):
    points = lobatto_points()
    result = np.ones((targets.shape[0], 4))
    for column in range(4):
        for second in range(4):
            if second != column:
                result[:, column] = (
                    result[:, column]
                    * (targets - points[second])
                    / (points[column] - points[second])
                )
    return result


def derivative_table():
    points = lobatto_points()
    result = np.zeros((4, 4))
    for row_at in range(4):
        for column in range(4):
            total = 0.0
            for skipped in range(4):
                if skipped != column:
                    factor = 1.0 / (points[column] - points[skipped])
                    for second in range(4):
                        if second != column and second != skipped:
                            factor = (
                                factor
                                * (points[row_at] - points[second])
                                / (points[column] - points[second])
                            )
                    total = total + factor
            result[row_at, column] = total
    return result


def cosine_table():
    index_list = np.arange(VSIDE)
    result = np.sqrt(2.0 / VSIDE) * np.cos(
        np.pi * (index_list[None, :] + 0.5) * index_list[:, None] / VSIDE
    )
    result[0] = result[0] / np.sqrt(2.0)
    return result


def static_tables():
    derivative = derivative_table()
    eye_four = np.eye(4)
    gradients = np.stack(
        [
            np.kron(np.kron(derivative, eye_four), eye_four),
            np.kron(np.kron(eye_four, derivative), eye_four),
            np.kron(np.kron(eye_four, eye_four), derivative),
        ]
    )
    selector = np.zeros((96, 64))
    for axis_at in range(3):
        for side_at in range(2):
            filled = 0
            for node_at in range(64):
                digits = (node_at // 16, node_at // 4 % 4, node_at % 4)
                if digits[axis_at] == 3 * side_at:
                    selector[(2 * axis_at + side_at) * 16 + filled, node_at] = 1.0
                    filled = filled + 1
    points = lobatto_points()
    halves = [lagrange_table((points - 1.0) / 2.0), lagrange_table((points + 1.0) / 2.0)]
    mortar = np.stack(
        [np.eye(16)]
        + [np.kron(halves[(which - 1) // 2], halves[(which - 1) % 2]) for which in range(1, 5)]
    )
    return (gradients, selector, mortar)


def velocity_components(first, count):
    index_list = first + jnp.arange(count)
    along = [index_list // (VSIDE * VSIDE), index_list // VSIDE % VSIDE, index_list % VSIDE]
    return jnp.stack([(entry.astype(jnp.float32) + 0.5) * (2.0 / VSIDE) - 1.0 for entry in along])


def collide_element(element, kernels, cosine, cosine_pair):
    width = element.shape[0]
    kernel_rows = kernels.shape[0]
    modes = (kernel_rows - 1) // 2
    values = element.astype(jnp.float32)
    cube = values.reshape(width, VSIDE, VSIDE * VSIDE)
    inner = jnp.einsum("nir,qr->niq", cube, cosine_pair, precision=highest)
    spectrum = jnp.einsum("ai,niq->naq", cosine, inner, precision=highest).reshape(width, 1, VEL)
    filtered = (spectrum * kernels[None]).reshape(width * kernel_rows, VSIDE, VSIDE * VSIDE)
    outer = jnp.einsum("ai,naq->niq", cosine, filtered, precision=highest)
    fields = jnp.einsum("niq,qr->nir", outer, cosine_pair, precision=highest).reshape(
        width, kernel_rows, VEL
    )
    gain = jnp.sum(fields[:, :modes] * fields[:, modes : 2 * modes], axis=1)
    loss = values * fields[:, 2 * modes]
    return (values + relax_step * (gain - loss)).astype(jnp.bfloat16)


def on_device(dist, send_faces, send_count, source_face, subface, alpha, beta):
    elements = dist.shape[0]
    vel_local = dist.shape[2]
    slots = send_faces.shape[2]
    gradients, selector, mortar = static_tables()
    grad_low = jnp.asarray(gradients, jnp.bfloat16)
    select_low = jnp.asarray(selector, jnp.bfloat16)
    select_full = jnp.asarray(selector, jnp.float32)
    mortar_low = jnp.asarray(mortar, jnp.bfloat16)
    speeds = velocity_components(lax.axis_index("vel") * vel_local, vel_local)
    rows = (
        jnp.einsum("tn,env->etv", select_low, dist, preferred_element_type=jnp.float32)
        .astype(jnp.bfloat16)
        .reshape(elements * 6, 16, vel_local)
    )
    picked = rows[send_faces[0].reshape(-1)].reshape(2, slots, 16, vel_local)
    live = jnp.arange(slots)[None, :] < send_count[0][:, None]
    outgoing = jnp.where(live[:, :, None, None], picked, jnp.zeros_like(picked))
    from_prev = passed_along(outgoing[1], "space", 1)
    from_next = passed_along(outgoing[0], "space", -1)
    drift = jnp.zeros(dist.shape, jnp.float32)
    for axis_at in range(3):
        drift = drift + speeds[axis_at] * jnp.einsum(
            "nm,emv->env", grad_low[axis_at], dist, preferred_element_type=jnp.float32
        )
    table = jnp.concatenate([rows, from_prev, from_next], axis=0)
    neighbour = table[source_face.reshape(-1)]
    projected = jnp.einsum(
        "ftu,fuv->ftv",
        mortar_low[subface.reshape(-1)],
        neighbour,
        preferred_element_type=jnp.float32,
    )
    inflow = jnp.minimum(
        jnp.stack([-speeds[0], speeds[0], -speeds[1], speeds[1], -speeds[2], speeds[2]]), 0.0
    )
    jump = (rows.astype(jnp.float32) - projected).reshape(elements, 6, 16, vel_local) * inflow[
        None, :, None, :
    ]
    lifted = jnp.einsum(
        "tn,etv->env", select_full, jump.reshape(elements, 96, vel_local), precision=highest
    )
    updated = (dist.astype(jnp.float32) - courant * drift + courant * lift_weight * lifted).astype(
        jnp.bfloat16
    )
    cosine_np = cosine_table()
    cosine = jnp.asarray(cosine_np, jnp.float32)
    cosine_pair = jnp.asarray(np.kron(cosine_np, cosine_np), jnp.float32)
    kernels = jnp.concatenate([alpha, beta], axis=0)

    def one_element(element):
        return collide_element(element, kernels, cosine, cosine_pair)

    mixed = lax.map(
        one_element, lax.all_to_all(updated, "vel", split_axis=1, concat_axis=2, tiled=True)
    )
    relaxed = lax.all_to_all(
        shortened(mixed), "vel", split_axis=2, concat_axis=1, tiled=True
    ).astype(mixed.dtype)
    return relaxed


def solution(mesh):
    return jax.shard_map(
        on_device,
        mesh=mesh,
        in_specs=(
            P("space", None, "vel"),
            P("space", None, None),
            P("space", None),
            P("space", None),
            P("space", None),
            P(),
            P(),
        ),
        out_specs=P("space", None, "vel"),
        check_vma=False,
    )
```

profile of v0, /device:TPU:1, one launch (start us, length us, event | category | flops | bytes accessed | tf_op | source)
XLA Modules:
  0.0 151.0 jit_solution(12709845251339062603)
XLA Ops:
  0.0 0.8 reshape_squeeze.3
  0.8 0.7 iota_compare_fusion
  1.6 1.4 convolution_convert_fusion
  3.7 4.0 %collective-permute-start = (bf16[16,16,256]{2,1,0:T(8,128)(2,1)S(1)}, bf16[16,16,256]{2,1,0:T(8,128)(2,1)S(1)}, u32[]{:S(2)}, u32[]{:S(2)}) collective-permute-start(bf16[16,16,256]{2,1,0:T(8,128)(2,1)S(1)} %get-tuple-element.63), channel_id=1, source_target_pairs={{496,0},{0,16},{16,32},{32,48},{48,64},{64,80},{80,96},{96,112},{1... | collective-permute-start | bytes 393224 | tf_op jit(solution)/shard_map/ppermute | solution.py:20
  7.7 11.7 %collective-permute-start.1 = (bf16[16,16,256]{2,1,0:T(8,128)(2,1)S(1)}, bf16[16,16,256]{2,1,0:T(8,128)(2,1)}, u32[]{:S(2)}, u32[]{:S(2)}) collective-permute-start(bf16[16,16,256]{2,1,0:T(8,128)(2,1)S(1)} %get-tuple-element.64), channel_id=1, source_target_pairs={{16,0},{32,16},{48,32},{64,48},{80,64},{96,80},{112,96},{128,112},... | collective-permute-start | bytes 393224 | tf_op jit(solution)/shard_map/ppermute | solution.py:20
  21.3 0.7 gather_fusion
  22.0 1.0 pad_maximum_fusion
  23.1 1.5 %gather_fusion.2 = bf16[96,16,256]{2,1,0:T(8,128)(2,1)} fusion(bf16[128,16,256]{2,1,0:T(8,128)(2,1)S(1)} %pad_maximum_fusion, s32[1024]{0:T(1024)S(1)} %pad_clamp_fusion), kind=kCustom, calls=%fused_computation.2 | custom fusion | bytes 1573248 | tf_op jit(solution)/shard_map/gather | solution.py:157
  24.6 1.5 convert_subtract_fusion
  26.8 1.2 fusion.13
  28.1 1.1 copy.25
  29.2 8.2 %all-to-all-start = ((bf16[16,64,256]{2,0,1:T(8,128)(2,1)}), bf16[16,64,256]{2,0,1:T(8,128)(2,1)S(1)}, u32[]{:S(2)}, u32[]{:S(2)}) async-start(bf16[16,64,256]{2,0,1:T(8,128)(2,1)} %copy.25), calls=%async_computation | async-start | bytes 1048576 | tf_op jit(solution)/shard_map/all_to_all | solution.py:185
  37.4 17.2 %all-to-all-done = bf16[16,64,256]{2,0,1:T(8,128)(2,1)S(1)} async-done(((bf16[16,64,256]{2,0,1:T(8,128)(2,1)}), bf16[16,64,256]{2,0,1:T(8,128)(2,1)S(1)}, u32[]{:S(2)}, u32[]{:S(2)}) %all-to-all-start) | async-done | bytes 524320 | tf_op jit(solution)/shard_map/all_to_all | solution.py:185
  54.7 54.8 %while.11 = (s32[]{:T(128)}, bf16[16,4,4096]{2,0,1:T(8,128)(2,1)S(1)}, bf16[16,4,4096]{2,0,1:T(8,128)(2,1)S(1)}, f32[9,4096]{1,0:T(8,128)S(1)}, s32[]{:T(128)}, ...) while((s32[]{:T(128)}, bf16[16,4,4096]{2,0,1:T(8,128)(2,1)S(1)}, ...), condition=%wide.region_2.3_spmd.clone, body=%wide.region_0.2_spmd.sunk.clone.sunk | while | flops 535134208 | bytes 7325801 | solution.py:184
  55.7 0.7 convolution_bitcast_fusion.5
  56.4 0.6 fusion.79
  57.5 0.7 dynamic_update_slice.7
  59.1 0.7 convolution_bitcast_fusion.5
  59.8 0.6 fusion.79
  60.9 0.7 dynamic_update_slice.7
  62.5 0.7 convolution_bitcast_fusion.5
  63.2 0.6 fusion.79
  64.3 0.7 dynamic_update_slice.7
  66.0 0.7 convolution_bitcast_fusion.5
  66.6 0.6 fusion.79
  67.8 0.7 dynamic_update_slice.7
  69.4 0.7 convolution_bitcast_fusion.5
  70.1 0.6 fusion.79
  71.2 0.7 dynamic_update_slice.7
  72.8 0.7 convolution_bitcast_fusion.5
  73.5 0.6 fusion.79
  74.6 0.7 dynamic_update_slice.7
  76.3 0.7 convolution_bitcast_fusion.5
  76.9 0.6 fusion.79
  78.1 0.7 dynamic_update_slice.7
  79.7 0.7 convolution_bitcast_fusion.5
  80.4 0.6 fusion.79
  81.5 0.7 dynamic_update_slice.7
  83.1 0.7 convolution_bitcast_fusion.5
  83.8 0.6 fusion.79
  84.9 0.7 dynamic_update_slice.7
  86.5 0.7 convolution_bitcast_fusion.5
  87.2 0.6 fusion.79
  88.3 0.7 dynamic_update_slice.7
  90.0 0.7 convolution_bitcast_fusion.5
  90.6 0.6 fusion.79
  91.8 0.7 dynamic_update_slice.7
  93.4 0.7 convolution_bitcast_fusion.5
  94.1 0.6 fusion.79
  95.2 0.7 dynamic_update_slice.7
  96.8 0.7 convolution_bitcast_fusion.5
  98.6 0.7 dynamic_update_slice.7
  100.3 0.7 convolution_bitcast_fusion.5
  102.0 0.7 dynamic_update_slice.7
  103.7 0.7 convolution_bitcast_fusion.5
  105.5 0.7 dynamic_update_slice.7
  107.1 0.7 convolution_bitcast_fusion.5
  108.9 0.7 dynamic_update_slice.7
  109.6 4.6 %copy.27 = bf16[16,4,4096]{0,1,2:T(4,128)(2,1)} copy(bf16[16,4,4096]{2,0,1:T(8,128)(2,1)S(1)} %get-tuple-element.37) | data formatting | bytes 1048576 | tf_op jit(solution)/shard_map/while | solution.py:184
  114.2 5.7 %reshape.472 = bf16[16,2,8192]{2,1,0:T(2,128)(2,1)S(1)} reshape(bf16[4096,4,16]{2,1,0:T(4,128)(2,1)} %bitcast.110) | data formatting | bytes 1048576
  119.9 20.0 %all_to_all.36 = bf16[16,2,8192]{2,1,0:T(2,128)(2,1)S(1)} all-to-all(bf16[16,2,8192]{2,1,0:T(2,128)(2,1)S(1)} %reshape.472), channel_id=1, replica_groups=mesh['space'=32,'vel'=16] {'vel'}, dimensions={0} | all-to-all | bytes 1048576 | tf_op jit(solution)/shard_map/all_to_all | solution.py:187
  139.9 4.1 %reshape.473 = bf16[4096,4,16]{2,1,0:T(4,128)(2,1)} reshape(bf16[16,2,8192]{2,1,0:T(2,128)(2,1)S(1)} %all_to_all.36) | data formatting | bytes 1048576
  144.1 6.0 %copy.28 = bf16[16,16,4,256]{3,2,1,0:T(4,128)(2,1)S(1)} copy(bf16[16,16,4,256]{0,2,3,1:T(4,128)(2,1)} %bitcast.111) | data formatting | bytes 1048576 | tf_op jit(solution)/shard_map/all_to_all | solution.py:187
  150.1 0.9 all_to_all.33
  (202 shorter events, 27.8 us)
Async XLA Ops:
  0.0 19.9 %copy-start.9 = (bf16[64,64,1]{1,0,2:T(8,128)(2,1)S(1)}, bf16[64,64,1]{1,0,2:T(8,128)(2,1)}, u32[]{:S(2)}) copy-start(bf16[64,64,1]{1,0,2:T(8,128)(2,1)} %constant.122) | copy-start | bytes 24580
  0.0 20.0 %copy-start.1 = (bf16[16,64,256]{2,1,0:T(8,128)(2,1)S(1)}, bf16[16,64,256]{2,1,0:T(8,128)(2,1)}, u32[]{:S(2)}) copy-start(bf16[16,64,256]{2,1,0:T(8,128)(2,1)} %param.15) | copy-start | bytes 1572868
  0.0 19.5 %copy-start.10 = (s32[16,6]{0,1:T(8,128)S(1)}, s32[16,6]{0,1:T(8,128)}, u32[]{:S(2)}) copy-start(s32[16,6]{0,1:T(8,128)} %param.18) | copy-start | bytes 1156
  0.0 19.7 %copy-start.11 = (s32[16,6]{0,1:T(8,128)S(1)}, s32[16,6]{0,1:T(8,128)}, u32[]{:S(2)}) copy-start(s32[16,6]{0,1:T(8,128)} %param.19) | copy-start | bytes 1156
  3.0 17.3 %copy-start.8 = (bf16[64,64,1]{1,0,2:T(8,128)(2,1)S(1)}, bf16[64,64,1]{1,0,2:T(8,128)(2,1)}, u32[]{:S(2)}) copy-start(bf16[64,64,1]{1,0,2:T(8,128)(2,1)} %constant.123) | copy-start | bytes 24580
  3.7 18.3 %collective-permute-start = (bf16[16,16,256]{2,1,0:T(8,128)(2,1)S(1)}, bf16[16,16,256]{2,1,0:T(8,128)(2,1)S(1)}, u32[]{:S(2)}, u32[]{:S(2)}) collective-permute-start(bf16[16,16,256]{2,1,0:T(8,128)(2,1)S(1)} %get-tuple-element.63), channel_id=1, source_target_pairs={{496,0},{0,16},{16,32},{32,48},{48,64},{64,80},{80,96},{96,112},{1... | collective-permute-start | bytes 393224 | tf_op jit(solution)/shard_map/ppermute | solution.py:20
  7.7 14.3 %collective-permute-start.1 = (bf16[16,16,256]{2,1,0:T(8,128)(2,1)S(1)}, bf16[16,16,256]{2,1,0:T(8,128)(2,1)}, u32[]{:S(2)}, u32[]{:S(2)}) collective-permute-start(bf16[16,16,256]{2,1,0:T(8,128)(2,1)S(1)} %get-tuple-element.64), channel_id=1, source_target_pairs={{16,0},{32,16},{48,32},{64,48},{80,64},{96,80},{112,96},{128,112},... | collective-permute-start | bytes 393224 | tf_op jit(solution)/shard_map/ppermute | solution.py:20
  20.3 0.7 copy-start.7
  20.6 0.7 copy-start.2
  26.1 0.8 copy-start.6
  28.1 9.3 %copy-start.4 = (f32[5,4096]{1,0:T(8,128)S(1)}, f32[5,4096]{1,0:T(8,128)}, u32[]{:S(2)}) copy-start(f32[5,4096]{1,0:T(8,128)} %param.21) | copy-start | bytes 245764
  28.1 9.3 %copy-start.5 = (f32[4,4096]{1,0:T(4,128)S(1)}, f32[4,4096]{1,0:T(4,128)}, u32[]{:S(2)}) copy-start(f32[4,4096]{1,0:T(4,128)} %param.20) | copy-start | bytes 196612
  28.1 26.6 %copy-start = (f32[256,256,1]{1,0,2:T(8,128)S(1)}, f32[256,256,1]{1,0,2:T(8,128)}, u32[]{:S(2)}) copy-start(f32[256,256,1]{1,0,2:T(8,128)} %constant.232) | copy-start | bytes 786436
  28.1 26.6 %copy-start.3 = (f32[16,16,1]{1,0,2:T(8,128)S(1)}, f32[16,16,1]{1,0,2:T(8,128)}, u32[]{:S(2)}) copy-start(f32[16,16,1]{1,0,2:T(8,128)} %constant.233) | copy-start | bytes 3076
  29.2 25.5 %all-to-all-start = ((bf16[16,64,256]{2,0,1:T(8,128)(2,1)}), bf16[16,64,256]{2,0,1:T(8,128)(2,1)S(1)}, u32[]{:S(2)}, u32[]{:S(2)}) async-start(bf16[16,64,256]{2,0,1:T(8,128)(2,1)} %copy.25), calls=%async_computation | async-start | bytes 1048576 | tf_op jit(solution)/shard_map/all_to_all | solution.py:185
where the time goes:
time: 152 us; the launch traced here: 151 us
  local copies, waits for them, and re-layouts  45.7 us (30%)
  matrix products  33.1 us (22%)
  starting transfers between devices  23.8 us (16%)
  blocking collectives  20 us (13%)
  waiting for transfers between devices  17.3 us (11%)
  other arithmetic  9.18 us (6%)
  loops' own time  1.55 us (1%)
    all_to_all x1, blocking collectives, on_device(): lax.all_to_all(shortened(mixed), 'vel', split_axis=2, concat_axis=1, tile...  20 us
    all_to_all x1, waiting for transfers between devices, on_device(): lax.all_to_all(updated, 'vel', split_axis=1, concat_axis=2, tiled=True)  17.2 us
    ppermute x2, starting transfers between devices, passed_along(): return lax.ppermute(block, axis, route)  15.6 us
    unnamed x28, local copies, waits for them, and re-layouts  11.1 us
    dynamic_update_slice x16, local copies, waits for them, and re-layouts, on_device(): lax.map(one_element, lax.all_to_all(updated, 'vel', split_axis=1, concat_...  10.7 us
    dot_general x16, matrix products, collide_element(): outer = jnp.einsum('ai,naq->niq', cosine, filtered, precision=highest)  10.6 us
    dot_general x16, matrix products, collide_element(): jnp.einsum('niq,qr->nir', outer, cosine_pair, precision=highest)  10.1 us
    all_to_all x1, starting transfers between devices, on_device(): lax.all_to_all(updated, 'vel', split_axis=1, concat_axis=2, tiled=True)  8.15 us
  transfers between devices with their start and end apart: 3, of which 1 were waited for; matrix products, arithmetic and copies ran while one was open for 1% of the time, Pallas kernels for 0%

commit v1 on v0

v1 whole, which is shorter than its diff:
```python
import jax
import jax.numpy as jnp
import ml_dtypes
import numpy as np
from jax import lax
from jax.experimental import pallas as pl
from jax.experimental.pallas import tpu as pltpu
from jax.sharding import PartitionSpec as P

VSIDE = 16
SLOTS = 16
GROUP = 16


courant = 0.1
lift_weight = 6.0
relax_step = 0.5


def passed_along(block, axis, distance):
    devices = range(lax.axis_size(axis))
    route = [((i - distance) % len(devices), i) for i in devices]
    return lax.ppermute(block, axis, route)


def lobatto_points():
    return np.array([-1.0, -1.0 / np.sqrt(5.0), 1.0 / np.sqrt(5.0), 1.0])


def lagrange_table(targets):
    points = lobatto_points()
    result = np.ones((targets.shape[0], 4))
    for column in range(4):
        for second in range(4):
            if second != column:
                result[:, column] = (
                    result[:, column]
                    * (targets - points[second])
                    / (points[column] - points[second])
                )
    return result


def derivative_table():
    points = lobatto_points()
    result = np.zeros((4, 4))
    for row_at in range(4):
        for column in range(4):
            total = 0.0
            for skipped in range(4):
                if skipped != column:
                    factor = 1.0 / (points[column] - points[skipped])
                    for second in range(4):
                        if second != column and second != skipped:
                            factor = (
                                factor
                                * (points[row_at] - points[second])
                                / (points[column] - points[second])
                            )
                    total = total + factor
            result[row_at, column] = total
    return result


def cosine_table():
    index_list = np.arange(VSIDE)
    result = np.sqrt(2.0 / VSIDE) * np.cos(
        np.pi * (index_list[None, :] + 0.5) * index_list[:, None] / VSIDE
    )
    result[0] = result[0] / np.sqrt(2.0)
    return result


def static_tables():
    derivative = derivative_table()
    eye_four = np.eye(4)
    gradients = np.stack(
        [
            np.kron(np.kron(derivative, eye_four), eye_four),
            np.kron(np.kron(eye_four, derivative), eye_four),
            np.kron(np.kron(eye_four, eye_four), derivative),
        ]
    )
    selector = np.zeros((96, 64))
    for axis_at in range(3):
        for side_at in range(2):
            filled = 0
            for node_at in range(64):
                digits = (node_at // 16, node_at // 4 % 4, node_at % 4)
                if digits[axis_at] == 3 * side_at:
                    selector[(2 * axis_at + side_at) * 16 + filled, node_at] = 1.0
                    filled = filled + 1
    points = lobatto_points()
    halves = [lagrange_table((points - 1.0) / 2.0), lagrange_table((points + 1.0) / 2.0)]
    mortar = np.stack(
        [np.eye(16)]
        + [np.kron(halves[(which - 1) // 2], halves[(which - 1) % 2]) for which in range(1, 5)]
    )
    return (gradients, selector, mortar)


def velocity_components(first, count):
    index_list = first + jnp.arange(count)
    along = [index_list // (VSIDE * VSIDE), index_list // VSIDE % VSIDE, index_list % VSIDE]
    return jnp.stack([(entry.astype(jnp.float32) + 0.5) * (2.0 / VSIDE) - 1.0 for entry in along])


def split_table(table):
    high = np.asarray(table, np.float32).astype(ml_dtypes.bfloat16)
    rest = np.asarray(table, np.float64) - high.astype(np.float64)
    return (high, np.asarray(rest, np.float32).astype(ml_dtypes.bfloat16))


def transport_tables():
    gradients, selector, mortar = static_tables()
    low = mortar.astype(np.float32).astype(ml_dtypes.bfloat16).astype(np.float64)
    tables = np.zeros((6, 5, 64, 256))
    for face in range(6):
        lift = selector[face * 16 : face * 16 + 16].T
        sign = -1.0 if face % 2 == 0 else 1.0
        for level in range(5):
            spread = sign * (lift @ low[level])
            tables[face, level, :, 64 + face * 16 : 80 + face * 16] = 4.0 * spread
            tables[face, level, :, 160 + face * 16 : 176 + face * 16] = 2.0 * spread
            if face % 2 == 0:
                tables[face, level, :, :64] = gradients[face // 2]
    return tables.astype(np.float32).astype(ml_dtypes.bfloat16)


def cosine_forward(values):
    count = len(values)
    if count == 1:
        return values
    half = count // 2
    sums = [values[i] + values[count - 1 - i] for i in range(half)]
    gaps = [
        (values[i] - values[count - 1 - i]) * float(0.5 / np.cos((i + 0.5) * np.pi / count))
        for i in range(half)
    ]
    even, odd = cosine_forward(sums), cosine_forward(gaps)
    result = []
    for i in range(half):
        result.append(even[i])
        result.append(odd[i] + odd[i + 1] if i + 1 < half else odd[i])
    return result


def cosine_backward(values):
    count = len(values)
    if count == 1:
        return values
    half = count // 2
    even = [values[2 * i] for i in range(half)]
    odd = [values[1]] + [values[2 * i - 1] + values[2 * i + 1] for i in range(1, half)]
    sums, gaps = cosine_backward(even), cosine_backward(odd)
    scaled = [gaps[i] * float(0.5 / np.cos((i + 0.5) * np.pi / count)) for i in range(half)]
    return [sums[i] + scaled[i] for i in range(half)] + [
        sums[half - 1 - i] - scaled[half - 1 - i] for i in range(half)
    ]


def dot(left, right):
    return jnp.dot(left, right, preferred_element_type=jnp.float32)


def send_kernel(faces_ref, count_ref, dist_ref, select_ref, back_ref, ahead_ref, rows):
    elements = dist_ref.shape[0]
    for at in range(elements):
        traces = dot(select_ref[...], dist_ref[at]).astype(jnp.bfloat16)
        rows[6 * at : 6 * at + 6] = traces.reshape(6, 16, dist_ref.shape[2])
    for way, out in enumerate((back_ref, ahead_ref)):
        for slot in range(SLOTS):
            trace = rows[faces_ref[way * SLOTS + slot]]
            keep = jnp.where(slot < count_ref[way], 1.0, 0.0).astype(jnp.bfloat16)
            out[slot] = trace * keep


def move_kernel(
    source_ref,
    level_ref,
    dist_ref,
    prev_ref,
    next_ref,
    select_ref,
    table_ref,
    mask_ref,
    speed_ref,
    keep_ref,
    out_ref,
    rows,
    stack,
):
    elements = dist_ref.shape[0]
    faces = 6 * elements
    for at in range(elements):
        traces = dot(select_ref[...], dist_ref[at]).astype(jnp.bfloat16)
        rows[6 * at : 6 * at + 6] = traces.reshape(6, 16, dist_ref.shape[2])
    rows[faces : faces + SLOTS] = prev_ref[...]
    rows[faces + SLOTS : faces + 2 * SLOTS] = next_ref[...]
    for at in range(elements):
        stack[at, :64] = dist_ref[at]
        for face in range(6):
            trace = rows[source_ref[6 * at + face]] * mask_ref[face]
            stack[at, 64 + 16 * face : 80 + 16 * face] = trace
            stack[at, 160 + 16 * face : 176 + 16 * face] = trace
        left = jnp.concatenate(
            [
                table_ref[2 * axis, level_ref[6 * at + 2 * axis]]
                + table_ref[2 * axis + 1, level_ref[6 * at + 2 * axis + 1]]
                for axis in range(3)
            ],
            axis=0,
        )
        moved = dot(left, stack[at])
        total = dist_ref[at].astype(jnp.float32) * keep_ref[...]
        for axis in range(3):
            total = total + moved[64 * axis : 64 * axis + 64] * speed_ref[axis : axis + 1, :]
        out_ref[at] = total.astype(jnp.bfloat16)


def collide_kernel(dist_ref, kern_ref, into_ref, back_ref, out_ref):
    nodes, plane = dist_ref.shape[1], dist_ref.shape[2]

    def planes(array):
        cube = array.reshape(VSIDE, nodes, plane)
        return [cube[i] for i in range(VSIDE)]

    values = dist_ref[...].reshape(VSIDE * nodes, plane)
    spectrum = cosine_forward(planes(dot(values, into_ref[0]) + dot(values, into_ref[1])))

    def field(which):
        filtered = jnp.concatenate(
            [
                (spectrum[i] * kern_ref[which, i : i + 1, :]).astype(jnp.bfloat16)
                for i in range(VSIDE)
            ],
            axis=0,
        )
        return cosine_backward(planes(dot(filtered, back_ref[0]) + dot(filtered, back_ref[1])))

    modes = (kern_ref.shape[0] - 1) // 2
    gain = None
    for mode in range(modes):
        first, second = field(mode), field(modes + mode)
        products = [a * b for a, b in zip(first, second)]
        gain = products if gain is None else [a + b for a, b in zip(gain, products)]
    loss = field(2 * modes)
    for i in range(VSIDE):
        value = dist_ref[i].astype(jnp.float32)
        out_ref[i] = (value + relax_step * (gain[i] - value * loss[i])).astype(jnp.bfloat16)


def in_vmem():
    return pl.BlockSpec(memory_space=pltpu.VMEM)


def in_smem():
    return pl.BlockSpec(memory_space=pltpu.SMEM)


def on_device(dist, send_faces, send_count, source_face, subface, alpha, beta):
    elements, nodes, vel_local = dist.shape
    faces = 6 * elements
    _, selector, _ = static_tables()
    select_low = jnp.asarray(selector, jnp.bfloat16)
    speeds = velocity_components(lax.axis_index("vel") * vel_local, vel_local)
    trace_shape = jax.ShapeDtypeStruct((SLOTS, 16, vel_local), jnp.bfloat16)

    back, ahead = pl.pallas_call(
        send_kernel,
        out_shape=(trace_shape, trace_shape),
        in_specs=[in_smem(), in_smem(), in_vmem(), in_vmem()],
        out_specs=(in_vmem(), in_vmem()),
        scratch_shapes=[pltpu.VMEM((faces, 16, vel_local), jnp.bfloat16)],
        name="send_traces",
    )(send_faces.reshape(-1), send_count.reshape(-1), dist, select_low)
    from_prev = passed_along(ahead, "space", 1)
    from_next = passed_along(back, "space", -1)

    on = jnp.stack([m for a in range(3) for m in (speeds[a] > 0.0, speeds[a] < 0.0)])
    masks = jnp.broadcast_to(on[:, None, :], (6, 16, vel_local)).astype(jnp.bfloat16)
    inflow = jnp.where(on, jnp.repeat(jnp.abs(speeds), 2, axis=0), 0.0)
    member = jnp.asarray(selector.reshape(6, 16, 64).sum(axis=1), jnp.float32)
    keep = 1.0 - courant * lift_weight * jnp.sum(member[:, :, None] * inflow[:, None, :], axis=0)
    updated = pl.pallas_call(
        move_kernel,
        out_shape=jax.ShapeDtypeStruct(dist.shape, jnp.bfloat16),
        in_specs=[in_smem(), in_smem()] + [in_vmem()] * 8,
        out_specs=in_vmem(),
        scratch_shapes=[
            pltpu.VMEM((faces + 2 * SLOTS, 16, vel_local), jnp.bfloat16),
            pltpu.VMEM((elements, 256, vel_local), jnp.bfloat16),
        ],
        name="transport",
    )(
        source_face.reshape(-1),
        subface.reshape(-1),
        dist,
        from_prev,
        from_next,
        select_low,
        jnp.asarray(transport_tables()),
        masks,
        -courant * speeds,
        keep,
    )

    plane = VSIDE * VSIDE
    cosine = cosine_table()
    pair = np.kron(cosine, cosine)
    into = jnp.asarray(np.stack(split_table(pair.T)))
    out_of = jnp.asarray(np.stack(split_table(pair)))
    norms = np.full((VSIDE, 1), 2.0 / VSIDE, np.float32)
    norms[0] = 1.0 / VSIDE
    kernels = jnp.concatenate([alpha, beta], axis=0).reshape(-1, VSIDE, plane) * norms
    gathered = lax.all_to_all(updated, "vel", split_axis=0, concat_axis=0, tiled=True)
    block = pl.BlockSpec((VSIDE, GROUP, plane), lambda g: (0, g, 0))
    mixed = pl.pallas_call(
        collide_kernel,
        out_shape=jax.ShapeDtypeStruct(gathered.shape, jnp.bfloat16),
        grid=(nodes // GROUP,),
        in_specs=[
            block,
            pl.BlockSpec(kernels.shape, lambda g: (0, 0, 0)),
            pl.BlockSpec(into.shape, lambda g: (0, 0, 0)),
            pl.BlockSpec(out_of.shape, lambda g: (0, 0, 0)),
        ],
        out_specs=block,
        name="collide",
    )(gathered, kernels, into, out_of)
    return lax.all_to_all(mixed, "vel", split_axis=0, concat_axis=0, tiled=True)


def solution(mesh):
    return jax.shard_map(
        on_device,
        mesh=mesh,
        in_specs=(
            P("space", None, "vel"),
            P("space", None, None),
            P("space", None),
            P("space", None),
            P("space", None),
            P(),
            P(),
        ),
        out_specs=P("space", None, "vel"),
        check_vma=False,
    )
```

time: 152 us -> 82.1 us (0.54)
  local copies, waits for them, and re-layouts: 45.7 us -> 6.57 us
  matrix products: 33.1 us -> 0 us
  Pallas kernels: 0 us -> 12.8 us
  other arithmetic: 9.18 us -> 2.25 us
  loops' own time: 1.55 us -> 0 us
    dot_general x70 -> x0, matrix products: 33.1 us -> none  [the longest x16 10.6 us: collide_element(): outer = jnp.einsum('ai,naq->niq', cosine, filtered, precision=highest)]
    pallas_call x0 -> x3, Pallas kernels: none -> 12.8 us  [the longest x1 7.29 us: on_device(): pl.pallas_call(collide_kernel, out_shape=jax.ShapeDtypeStruct(gathered.sh...]
    dynamic_update_slice x16 -> x0, local copies, waits for them, and re-layouts: 10.7 us -> none  [on_device(): lax.map(one_element, lax.all_to_all(updated, 'vel', split_axis=1, concat_...]
    unnamed x28 -> x22, local copies, waits for them, and re-layouts: 11.1 us -> 3.28 us
    all_to_all x3 -> x0, local copies, waits for them, and re-layouts: 6.98 us -> none  [the longest x2 6.95 us: on_device(): lax.all_to_all(shortened(mixed), 'vel', split_axis=2, concat_axis=1, tile...]
    while x17 -> x0, local copies, waits for them, and re-layouts: 5.33 us -> none  [the longest x1 4.6 us: on_device(): lax.map(one_element, lax.all_to_all(updated, 'vel', split_axis=1, concat_...]
    reduce_sum x16 -> x1, other arithmetic: 3.47 us -> 0.11 us  [on_device(): jnp.sum(member[:, :, None] * inflow[:, None, :], axis=0)]
    dynamic_slice x16 -> x0, local copies, waits for them, and re-layouts: 3.29 us -> none  [on_device(): lax.map(one_element, lax.all_to_all(updated, 'vel', split_axis=1, concat_...]
  transfers between devices with their start and end apart: 3 -> 3, of which waited for: 1 -> 1; matrix products, arithmetic and copies ran while one was open for 1% -> 5% of each run, Pallas kernels for 0% -> 0%
where the time goes in v1:
time: 82.1 us; the launch traced here: 81.5 us
  starting transfers between devices  23.8 us (29%)
  blocking collectives  20.2 us (25%)
  waiting for transfers between devices  15.8 us (19%)
  Pallas kernels  12.8 us (16%)
  local copies, waits for them, and re-layouts  6.57 us (8%)
  other arithmetic  2.25 us (3%)
    all_to_all x1, blocking collectives, on_device(): return lax.all_to_all(mixed, 'vel', split_axis=0, concat_axis=0, tiled=True)  20.2 us
    all_to_all x1, waiting for transfers between devices, on_device(): lax.all_to_all(updated, 'vel', split_axis=0, concat_axis=0, tiled=True)  15.8 us
    ppermute x2, starting transfers between devices, passed_along(): return lax.ppermute(block, axis, route)  15.6 us
    all_to_all x1, starting transfers between devices, on_device(): lax.all_to_all(updated, 'vel', split_axis=0, concat_axis=0, tiled=True)  8.22 us
    pallas_call x1, Pallas kernels, on_device(): pl.pallas_call(collide_kernel, out_shape=jax.ShapeDtypeStruct(gathered.sh...  7.29 us
    pallas_call x1, Pallas kernels, on_device(): pl.pallas_call(move_kernel, out_shape=jax.ShapeDtypeStruct(dist.shape, jn...  3.4 us
    unnamed x22, local copies, waits for them, and re-layouts  3.28 us
    pallas_call x1, Pallas kernels, on_device(): pl.pallas_call(send_kernel, out_shape=(trace_shape, trace_shape), in_spec...  2.13 us
  transfers between devices with their start and end apart: 3, of which 1 were waited for; matrix products, arithmetic and copies ran while one was open for 5% of the time, Pallas kernels for 0%

profile of v1, /device:TPU:1, one launch (start us, length us, event | category | flops | bytes accessed | tf_op | source)
XLA Modules:
  0.0 81.5 jit_solution(6158826533049306093)
XLA Ops:
  0.0 1.3 %reshape.260.faces_ref = s32[32]{0:T(128)} reshape(s32[1,2,16]{2,1,0:T(2,128)} %param.14) | data formatting | bytes 256 | tf_op jit(solution)/shard_map/reshape | solution.py:276
  1.3 2.1 %send_traces.1 = (bf16[16,16,256]{2,1,0:T(8,128)(2,1)}, bf16[16,16,256]{2,1,0:T(8,128)(2,1)}) custom-call(s32[32]{0:T(128)} %reshape.260.faces_ref, s32[2]{0:T(128)} %bitcast.6, bf16[16,64,256]{2,1,0:T(8,128)(2,1)} %dist_ref.3, bf16[96,64]{1,0:T(8,128)(2,1)} %constant.79.clone.select_ref), custom_call_target="tpu_custom_call" | custom-call | tf_op jit(solution)/shard_map/send_traces/pallas_call | solution.py:269
  3.4 3.9 %collective-permute-start = (bf16[16,16,256]{2,1,0:T(8,128)(2,1)}, bf16[16,16,256]{2,1,0:T(8,128)(2,1)S(1)}, u32[]{:S(2)}, u32[]{:S(2)}) collective-permute-start(bf16[16,16,256]{2,1,0:T(8,128)(2,1)} %get-tuple-element.7), channel_id=1, source_target_pairs={{496,0},{0,16},{16,32},{32,48},{48,64},{64,80},{80,96},{96,112},{1... | collective-permute-start | bytes 393224 | tf_op jit(solution)/shard_map/ppermute | solution.py:23
  7.3 11.7 %collective-permute-start.1 = (bf16[16,16,256]{2,1,0:T(8,128)(2,1)}, bf16[16,16,256]{2,1,0:T(8,128)(2,1)S(1)}, u32[]{:S(2)}, u32[]{:S(2)}) collective-permute-start(bf16[16,16,256]{2,1,0:T(8,128)(2,1)} %get-tuple-element.8), channel_id=1, source_target_pairs={{16,0},{32,16},{48,32},{64,48},{80,64},{96,80},{112,96},{128,112},... | collective-permute-start | bytes 393224 | tf_op jit(solution)/shard_map/ppermute | solution.py:23
  19.2 0.6 fusion
  19.8 0.0 copy-start.5
  19.8 0.7 copy-done.5
  20.5 0.1 copy.18
  20.6 0.0 copy-start.6
  20.6 0.7 reshape.258.source_ref
  21.2 0.0 copy-done.6
  21.3 0.1 copy.19
  21.3 0.0 copy-start.7
  21.3 0.6 reshape.259.level_ref
  22.0 0.1 copy-done.7
  22.0 0.1 multiply_reduce_fusion
  22.1 0.6 multiply_subtract_fusion.keep_ref
  22.8 0.0 collective-permute-done.prev_ref
  22.8 0.0 copy-start.2
  22.8 0.0 collective-permute-done.1.next_ref
  22.8 0.0 copy-start.3
  22.8 0.7 broadcast_in_dim.8.mask_ref
  23.5 0.0 copy-done.2
  23.5 0.0 copy-done.3
  23.5 3.4 %transport.1 = bf16[16,64,256]{2,1,0:T(8,128)(2,1)} custom-call(s32[96]{0:T(128)} %reshape.258.source_ref, s32[96]{0:T(128)} %reshape.259.level_ref, bf16[16,64,256]{2,1,0:T(8,128)(2,1)} %dist_ref.3, bf16[16,16,256]{2,1,0:T(8,128)(2,1)} %copy-done.2, bf16[16,16,256]{2,1,0:T(8,128)(2,1)} %copy-done.3, bf16[96,64]{1,0:T(8,128)(2,1)} %constant.79.clone.select_ref, ...), custom_call_target="tpu_custom_call" | custom-call | tf_op jit(solution)/shard_map/transport/pallas_call | solution.py:285
  26.9 0.0 copy-start.1
  26.9 0.0 copy-start.4
  26.9 8.2 %all-to-all-start = ((bf16[16,64,256]{2,1,0:T(8,128)(2,1)}), bf16[16,64,256]{2,1,0:T(8,128)(2,1)S(1)}, u32[]{:S(2)}, u32[]{:S(2)}) async-start(bf16[16,64,256]{2,1,0:T(8,128)(2,1)} %transport.1), calls=%async_computation | async-start | bytes 1048576 | tf_op jit(solution)/shard_map/all_to_all | solution.py:316
  35.1 0.0 copy-done.1
  35.1 0.0 copy-done.4
  35.2 0.1 copy.20
  35.3 0.0 copy-start.8
  35.3 0.6 copy-done.8
  36.0 0.7 slice_multiply_fusion.kern_ref
  36.7 15.8 %all-to-all-done.dist_ref = bf16[16,64,256]{2,1,0:T(8,128)(2,1)S(1)} async-done(((bf16[16,64,256]{2,1,0:T(8,128)(2,1)}), bf16[16,64,256]{2,1,0:T(8,128)(2,1)S(1)}, u32[]{:S(2)}, u32[]{:S(2)}) %all-to-all-start) | async-done | bytes 524320 | tf_op jit(solution)/shard_map/all_to_all | solution.py:316
  52.5 0.0 copy-start
  52.5 0.8 copy-done
  53.3 7.3 %collide.1 = bf16[16,64,256]{2,1,0:T(8,128)(2,1)} custom-call(bf16[16,64,256]{2,1,0:T(8,128)(2,1)} %copy-done, f32[9,16,256]{2,1,0:T(8,128)} %slice_multiply_fusion.kern_ref, bf16[2,256,256]{2,1,0:T(8,128)(2,1)} %constant.82.clone.into_ref, bf16[2,256,256]{2,1,0:T(8,128)(2,1)} %constant.83.clone.back_ref), custom_call_target="tpu_custom_call" | custom-call | tf_op jit(solution)/shard_map/collide/pallas_call | solution.py:318
  60.5 20.2 %all_to_all.10 = bf16[16,64,256]{2,1,0:T(8,128)(2,1)S(1)} all-to-all(bf16[16,64,256]{2,1,0:T(8,128)(2,1)} %collide.1), channel_id=1, replica_groups=mesh['space'=32,'vel'=16] {'vel'}, dimensions={0} | all-to-all | bytes 1048576 | tf_op jit(solution)/shard_map/all_to_all | solution.py:331
  80.7 0.8 copy.22
  (11 shorter events, 0.2 us)
Async XLA Ops:
  3.4 19.4 %collective-permute-start = (bf16[16,16,256]{2,1,0:T(8,128)(2,1)}, bf16[16,16,256]{2,1,0:T(8,128)(2,1)S(1)}, u32[]{:S(2)}, u32[]{:S(2)}) collective-permute-start(bf16[16,16,256]{2,1,0:T(8,128)(2,1)} %get-tuple-element.7), channel_id=1, source_target_pairs={{496,0},{0,16},{16,32},{32,48},{48,64},{64,80},{80,96},{96,112},{1... | collective-permute-start | bytes 393224 | tf_op jit(solution)/shard_map/ppermute | solution.py:23
  7.3 15.5 %collective-permute-start.1 = (bf16[16,16,256]{2,1,0:T(8,128)(2,1)}, bf16[16,16,256]{2,1,0:T(8,128)(2,1)S(1)}, u32[]{:S(2)}, u32[]{:S(2)}) collective-permute-start(bf16[16,16,256]{2,1,0:T(8,128)(2,1)} %get-tuple-element.8), channel_id=1, source_target_pairs={{16,0},{32,16},{48,32},{64,48},{80,64},{96,80},{112,96},{128,112},... | collective-permute-start | bytes 393224 | tf_op jit(solution)/shard_map/ppermute | solution.py:23
  19.8 0.7 copy-start.5
  20.6 0.7 copy-start.6
  21.3 0.7 copy-start.7
  22.8 0.7 copy-start.2
  22.8 0.7 copy-start.3
  26.9 8.2 %copy-start.1 = (f32[5,4096]{1,0:T(8,128)S(1)}, f32[5,4096]{1,0:T(8,128)}, u32[]{:S(2)}) copy-start(f32[5,4096]{1,0:T(8,128)} %param.19) | copy-start | bytes 245764
  26.9 8.2 %copy-start.4 = (f32[4,4096]{1,0:T(4,128)S(1)}, f32[4,4096]{1,0:T(4,128)}, u32[]{:S(2)}) copy-start(f32[4,4096]{1,0:T(4,128)} %param.18) | copy-start | bytes 196612
  26.9 25.5 %all-to-all-start = ((bf16[16,64,256]{2,1,0:T(8,128)(2,1)}), bf16[16,64,256]{2,1,0:T(8,128)(2,1)S(1)}, u32[]{:S(2)}, u32[]{:S(2)}) async-start(bf16[16,64,256]{2,1,0:T(8,128)(2,1)} %transport.1), calls=%async_computation | async-start | bytes 1048576 | tf_op jit(solution)/shard_map/all_to_all | solution.py:316
  35.3 0.7 copy-start.8
  52.5 0.8 copy-start

commit v2 on v1

v2 whole, which is shorter than its diff:
```python
import jax
import jax.numpy as jnp
import ml_dtypes
import numpy as np
from jax import lax
from jax.experimental import pallas as pl
from jax.experimental.pallas import tpu as pltpu
from jax.sharding import PartitionSpec as P

VSIDE = 16
SLOTS = 16
GROUP = 16
PIECES = 4


courant = 0.1
lift_weight = 6.0
relax_step = 0.5


def passed_along(block, axis, distance):
    devices = range(lax.axis_size(axis))
    route = [((i - distance) % len(devices), i) for i in devices]
    return lax.ppermute(block, axis, route)


def lobatto_points():
    return np.array([-1.0, -1.0 / np.sqrt(5.0), 1.0 / np.sqrt(5.0), 1.0])


def lagrange_table(targets):
    points = lobatto_points()
    result = np.ones((targets.shape[0], 4))
    for column in range(4):
        for second in range(4):
            if second != column:
                result[:, column] = (
                    result[:, column]
                    * (targets - points[second])
                    / (points[column] - points[second])
                )
    return result


def derivative_table():
    points = lobatto_points()
    result = np.zeros((4, 4))
    for row_at in range(4):
        for column in range(4):
            total = 0.0
            for skipped in range(4):
                if skipped != column:
                    factor = 1.0 / (points[column] - points[skipped])
                    for second in range(4):
                        if second != column and second != skipped:
                            factor = (
                                factor
                                * (points[row_at] - points[second])
                                / (points[column] - points[second])
                            )
                    total = total + factor
            result[row_at, column] = total
    return result


def cosine_table():
    index_list = np.arange(VSIDE)
    result = np.sqrt(2.0 / VSIDE) * np.cos(
        np.pi * (index_list[None, :] + 0.5) * index_list[:, None] / VSIDE
    )
    result[0] = result[0] / np.sqrt(2.0)
    return result


def static_tables():
    derivative = derivative_table()
    eye_four = np.eye(4)
    gradients = np.stack(
        [
            np.kron(np.kron(derivative, eye_four), eye_four),
            np.kron(np.kron(eye_four, derivative), eye_four),
            np.kron(np.kron(eye_four, eye_four), derivative),
        ]
    )
    selector = np.zeros((96, 64))
    for axis_at in range(3):
        for side_at in range(2):
            filled = 0
            for node_at in range(64):
                digits = (node_at // 16, node_at // 4 % 4, node_at % 4)
                if digits[axis_at] == 3 * side_at:
                    selector[(2 * axis_at + side_at) * 16 + filled, node_at] = 1.0
                    filled = filled + 1
    points = lobatto_points()
    halves = [lagrange_table((points - 1.0) / 2.0), lagrange_table((points + 1.0) / 2.0)]
    mortar = np.stack(
        [np.eye(16)]
        + [np.kron(halves[(which - 1) // 2], halves[(which - 1) % 2]) for which in range(1, 5)]
    )
    return (gradients, selector, mortar)


def split_table(table):
    high = np.asarray(table, np.float32).astype(ml_dtypes.bfloat16)
    rest = np.asarray(table, np.float64) - high.astype(np.float64)
    return (high, np.asarray(rest, np.float32).astype(ml_dtypes.bfloat16))


def mortar_lifts():
    _, selector, mortar = static_tables()
    tables = np.zeros((6, 5, 64, 128))
    for face in range(6):
        lift = selector[face * 16 : face * 16 + 16].T
        sign = -1.0 if face % 2 == 0 else 1.0
        for level in range(5):
            tables[face, level, :, face * 16 : face * 16 + 16] = sign * (lift @ mortar[level])
    return tables.astype(np.float32).astype(ml_dtypes.bfloat16)


def cosine_forward(values):
    count = len(values)
    if count == 1:
        return values
    half = count // 2
    sums = [values[i] + values[count - 1 - i] for i in range(half)]
    gaps = [
        (values[i] - values[count - 1 - i]) * float(0.5 / np.cos((i + 0.5) * np.pi / count))
        for i in range(half)
    ]
    even, odd = cosine_forward(sums), cosine_forward(gaps)
    result = []
    for i in range(half):
        result.append(even[i])
        result.append(odd[i] + odd[i + 1] if i + 1 < half else odd[i])
    return result


def cosine_backward(values):
    count = len(values)
    if count == 1:
        return values
    half = count // 2
    even = [values[2 * i] for i in range(half)]
    odd = [values[1]] + [values[2 * i - 1] + values[2 * i + 1] for i in range(1, half)]
    sums, gaps = cosine_backward(even), cosine_backward(odd)
    scaled = [gaps[i] * float(0.5 / np.cos((i + 0.5) * np.pi / count)) for i in range(half)]
    return [sums[i] + scaled[i] for i in range(half)] + [
        sums[half - 1 - i] - scaled[half - 1 - i] for i in range(half)
    ]


def dot(left, right):
    return jnp.dot(left, right, preferred_element_type=jnp.float32)


def face_nodes(face, shape, along):
    at = lax.broadcasted_iota(jnp.int32, shape, along)
    axis, side = face // 2, face % 2
    if axis == 0:
        return at + 48 * side
    high, low = at >> 2, at & 3
    return 16 * high + 12 * side + low if axis == 1 else 16 * high + 4 * low + 3 * side


def local_speeds(shape):
    index = lax.axis_index("vel") * shape[-1] + lax.broadcasted_iota(jnp.int32, shape, len(shape) - 1)
    along = [index // (VSIDE * VSIDE), (index // VSIDE) & (VSIDE - 1), index & (VSIDE - 1)]
    return [(entry.astype(jnp.float32) + 0.5) * (2.0 / VSIDE) - 1.0 for entry in along]


def inflow_faces(speeds):
    return [speeds[f // 2] > 0.0 if f % 2 == 0 else speeds[f // 2] < 0.0 for f in range(6)]


def inflow_masks(shape):
    ones = [jnp.where(on, 1.0, 0.0) for on in inflow_faces(local_speeds(shape))]
    return [one.astype(jnp.bfloat16) for one in ones]


def send_kernel(faces_ref, count_ref, dist_ref, back_ref, ahead_ref, held, rows, sems):
    elements, nodes, width = held.shape
    step = elements // PIECES

    def piece(at):
        part = pl.ds(at * step, step)
        return pltpu.make_async_copy(dist_ref.at[part], held.at[part], sems.at[at])

    for at in range(PIECES):
        piece(at).start()
    node = lax.broadcasted_iota(jnp.int32, (16, nodes), 1)
    select = jnp.concatenate(
        [jnp.where(face_nodes(f, (16, nodes), 0) == node, 1.0, 0.0) for f in range(6)], axis=0
    ).astype(jnp.bfloat16)
    for at in range(elements):
        if at % step == 0:
            piece(at // step).wait()
        traces = dot(select, held[at]).astype(jnp.bfloat16)
        rows[6 * at : 6 * at + 6] = traces.reshape(6, 16, width)
    for way, out in enumerate((back_ref, ahead_ref)):
        for slot in range(SLOTS):
            trace = rows[faces_ref[0, way, slot]]
            keep = jnp.where(slot < count_ref[0, way], 1.0, 0.0).astype(jnp.bfloat16)
            out[slot] = trace * keep


def lift_traces(at, level_ref, lift_ref, stack, total):
    speeds = local_speeds((1, total.shape[-1]))
    left = jnp.concatenate(
        [
            lift_ref[2 * axis, level_ref[2 * axis, at]]
            + lift_ref[2 * axis + 1, level_ref[2 * axis + 1, at]]
            for axis in range(3)
        ],
        axis=0,
    )
    lifted = dot(left, stack[at])
    for axis in range(3):
        weight = -courant * lift_weight * speeds[axis]
        total = total + lifted[64 * axis : 64 * axis + 64] * weight
    return total


def local_kernel(source_ref, level_ref, held, rows, gradient_ref, lift_ref, out_ref, table, stack):
    elements, nodes, width = held.shape
    faces = 6 * elements
    table[:faces] = rows[...]
    table[faces] = jnp.zeros((16, width), jnp.bfloat16)
    speeds = local_speeds((1, width))
    masks = inflow_masks((16, width))
    wide = local_speeds((nodes, width))
    node = lax.broadcasted_iota(jnp.int32, (nodes, width), 0)
    digits = [node >> 4, (node >> 2) & 3, node & 3]
    loss = jnp.zeros((nodes, width), jnp.float32)
    for face, on in enumerate(inflow_faces(wide)):
        member = jnp.logical_and(on, digits[face // 2] == 3 * (face % 2))
        loss = loss + jnp.where(member, jnp.abs(wide[face // 2]), 0.0)
    keep = 1.0 - courant * lift_weight * loss
    for at in range(elements):
        for face in range(6):
            trace = table[jnp.minimum(source_ref[face, at], faces)] * masks[face]
            stack[at, 16 * face : 16 * face + 16] = trace
        stack[at, 96:] = jnp.zeros((32, width), jnp.bfloat16)
        total = held[at].astype(jnp.float32) * keep
        moved = dot(gradient_ref[...], held[at])
        for axis in range(3):
            total = total + moved[64 * axis : 64 * axis + 64] * (-courant * speeds[axis])
        out_ref[at] = lift_traces(at, level_ref, lift_ref, stack, total)


def remote_kernel(source_ref, level_ref, part_ref, prev_ref, next_ref, lift_ref, out_ref, table, stack):
    elements, _, width = part_ref.shape
    faces = 6 * elements
    table[0] = jnp.zeros((16, width), jnp.bfloat16)
    table[1 : SLOTS + 1] = prev_ref[...]
    table[SLOTS + 1 :] = next_ref[...]
    masks = inflow_masks((16, width))
    for at in range(elements):
        for face in range(6):
            trace = table[jnp.maximum(source_ref[face, at] - (faces - 1), 0)] * masks[face]
            stack[at, 16 * face : 16 * face + 16] = trace
        stack[at, 96:] = jnp.zeros((32, width), jnp.bfloat16)
        total = lift_traces(at, level_ref, lift_ref, stack, part_ref[at])
        out_ref[at] = total.astype(jnp.bfloat16)


def collide_kernel(dist_ref, kern_ref, into_ref, back_ref, out_ref, spectrum, fields, first, gain):
    nodes, plane = dist_ref.shape[1], dist_ref.shape[2]
    modes = (kern_ref.shape[0] - 1) // 2
    order = [m for pair in range(modes) for m in (pair, modes + pair)] + [2 * modes]
    halves = [slice(0, plane // 2), slice(plane // 2, plane)]

    def planes(slot, lanes):
        return [fields[slot, i * GROUP : (i + 1) * GROUP, lanes] for i in range(VSIDE)]

    for start in range(0, nodes, GROUP):
        group = slice(start, start + GROUP)
        values = dist_ref[:, group, :].reshape(VSIDE * GROUP, plane)
        fields[0] = dot(values, into_ref[0]) + dot(values, into_ref[1])
        for lanes in halves:
            for i, part in enumerate(cosine_forward(planes(0, lanes))):
                spectrum[i, :, lanes] = part

        def filtered(which, slot):
            parts = [
                (spectrum[i] * kern_ref[which, i : i + 1, :]).astype(jnp.bfloat16)
                for i in range(VSIDE)
            ]
            left = jnp.concatenate(parts, axis=0)
            fields[slot] = dot(left, back_ref[0]) + dot(left, back_ref[1])

        def gathered(which, slot):
            for lanes in halves:
                for i, field in enumerate(cosine_backward(planes(slot, lanes))):
                    if which < modes:
                        first[i, :, lanes] = field
                    elif which == modes:
                        gain[i, :, lanes] = first[i, :, lanes] * field
                    elif which < 2 * modes:
                        gain[i, :, lanes] = gain[i, :, lanes] + first[i, :, lanes] * field
                    else:
                        value = dist_ref[i, group, lanes].astype(jnp.float32)
                        total = value + relax_step * (gain[i, :, lanes] - value * field)
                        out_ref[i, group, lanes] = total.astype(jnp.bfloat16)

        filtered(order[0], 0)
        for at, which in enumerate(order):
            if at + 1 < len(order):
                filtered(order[at + 1], (at + 1) % 2)
            gathered(which, at % 2)


def in_vmem():
    return pl.BlockSpec(memory_space=pltpu.VMEM)


def in_smem():
    return pl.BlockSpec(memory_space=pltpu.SMEM)


def on_chip(array):
    return pltpu.with_memory_space_constraint(array, pltpu.VMEM)


def on_device(dist, send_faces, send_count, source_face, subface, alpha, beta):
    elements, nodes, width = dist.shape
    faces = 6 * elements
    gradients, _, _ = static_tables()
    traces = pltpu.VMEM((SLOTS, 16, width), jnp.bfloat16)

    back, ahead, held, rows = pl.pallas_call(
        send_kernel,
        out_shape=(
            traces,
            traces,
            pltpu.VMEM(dist.shape, jnp.bfloat16),
            pltpu.VMEM((faces, 16, width), jnp.bfloat16),
        ),
        in_specs=[in_smem(), in_smem(), pl.BlockSpec(memory_space=pl.ANY)],
        out_specs=(in_vmem(),) * 4,
        scratch_shapes=[pltpu.SemaphoreType.DMA((PIECES,))],
        name="send_traces",
    )(send_faces, send_count, dist)
    from_prev = passed_along(ahead, "space", 1)
    from_next = passed_along(back, "space", -1)

    sources, levels = source_face.T, subface.T
    lifts = on_chip(jnp.asarray(mortar_lifts()))
    gradient = on_chip(jnp.asarray(gradients.reshape(3 * nodes, nodes), jnp.bfloat16))
    part = pl.pallas_call(
        local_kernel,
        out_shape=pltpu.VMEM(dist.shape, jnp.float32),
        in_specs=[in_smem(), in_smem()] + [in_vmem()] * 4,
        out_specs=in_vmem(),
        scratch_shapes=[
            pltpu.VMEM((faces + 1, 16, width), jnp.bfloat16),
            pltpu.VMEM((elements, 128, width), jnp.bfloat16),
        ],
        name="transport_local",
    )(sources, levels, on_chip(held), on_chip(rows), gradient, lifts)
    updated = pl.pallas_call(
        remote_kernel,
        out_shape=pltpu.VMEM(dist.shape, jnp.bfloat16),
        in_specs=[in_smem(), in_smem()] + [in_vmem()] * 4,
        out_specs=in_vmem(),
        scratch_shapes=[
            pltpu.VMEM((2 * SLOTS + 1, 16, width), jnp.bfloat16),
            pltpu.VMEM((elements, 128, width), jnp.bfloat16),
        ],
        name="transport_remote",
    )(sources, levels, on_chip(part), on_chip(from_prev), on_chip(from_next), lifts)

    plane = VSIDE * VSIDE
    cosine = cosine_table()
    pair = np.kron(cosine, cosine)
    into = on_chip(jnp.asarray(np.stack(split_table(pair.T))))
    out_of = on_chip(jnp.asarray(np.stack(split_table(pair))))
    norms = np.full((VSIDE, 1), 2.0 / VSIDE, np.float32)
    norms[0] = 1.0 / VSIDE
    kernels = jnp.concatenate([alpha, beta], axis=0).reshape(-1, VSIDE, plane) * norms
    whole = lax.all_to_all(updated, "vel", split_axis=0, concat_axis=0, tiled=True)
    cube = pltpu.VMEM((VSIDE, GROUP, plane), jnp.float32)
    mixed = pl.pallas_call(
        collide_kernel,
        out_shape=pltpu.VMEM(whole.shape, jnp.bfloat16),
        in_specs=[in_vmem()] * 4,
        out_specs=in_vmem(),
        scratch_shapes=[cube, pltpu.VMEM((2, VSIDE * GROUP, plane), jnp.float32), cube, cube],
        name="collide",
    )(on_chip(whole), on_chip(kernels), into, out_of)
    return lax.all_to_all(mixed, "vel", split_axis=0, concat_axis=0, tiled=True)


def solution(mesh):
    return jax.shard_map(
        on_device,
        mesh=mesh,
        in_specs=(
            P("space", None, "vel"),
            P("space", None, None),
            P("space", None),
            P("space", None),
            P("space", None),
            P(),
            P(),
        ),
        out_specs=P("space", None, "vel"),
        check_vma=False,
    )
```

time: 82.1 us -> 79.6 us (0.970)
  other arithmetic: 2.25 us -> 0.12 us
    unnamed x22 -> x26, local copies, waits for them, and re-layouts: 3.28 us -> 6.32 us
    reshape x4 -> x0, local copies, waits for them, and re-layouts: 2.57 us -> none  [the longest x1 1.28 us: on_device(): send_faces.reshape(-1)]
    pallas_call x3 -> x4, Pallas kernels: 12.8 us -> 12.1 us  [the longest x1 4.89 us: on_device(): pl.pallas_call(collide_kernel, out_shape=pltpu.VMEM(whole.shape, jnp.bflo...]
  transfers between devices with their start and end apart: 3 -> 3, of which waited for: 1 -> 1; matrix products, arithmetic and copies ran while one was open for 5% -> 0% of each run, Pallas kernels for 0% -> 2%
where the time goes in v2:
time: 79.6 us; the launch traced here: 79.1 us
  starting transfers between devices  23.8 us (30%)
  blocking collectives  20 us (25%)
  waiting for transfers between devices  16.5 us (21%)
  Pallas kernels  12.1 us (15%)
  local copies, waits for them, and re-layouts  6.32 us (8%)
    all_to_all x1, blocking collectives, on_device(): return lax.all_to_all(mixed, 'vel', split_axis=0, concat_axis=0, tiled=True)  20 us
    all_to_all x1, waiting for transfers between devices, on_device(): lax.all_to_all(updated, 'vel', split_axis=0, concat_axis=0, tiled=True)  16.5 us
    ppermute x2, starting transfers between devices, passed_along(): return lax.ppermute(block, axis, route)  15.6 us
    all_to_all x1, starting transfers between devices, on_device(): lax.all_to_all(updated, 'vel', split_axis=0, concat_axis=0, tiled=True)  8.2 us
    unnamed x26, local copies, waits for them, and re-layouts  6.32 us
    pallas_call x1, Pallas kernels, on_device(): pl.pallas_call(collide_kernel, out_shape=pltpu.VMEM(whole.shape, jnp.bflo...  4.89 us
    pallas_call x1, Pallas kernels, on_device(): pl.pallas_call(send_kernel, out_shape=(traces, traces, pltpu.VMEM(dist.sh...  3.18 us
    pallas_call x1, Pallas kernels, on_device(): pl.pallas_call(remote_kernel, out_shape=pltpu.VMEM(dist.shape, jnp.bfloat...  2.22 us
  transfers between devices with their start and end apart: 3, of which 1 were waited for; matrix products, arithmetic and copies ran while one was open for 0% of the time, Pallas kernels for 2%

profile of v2, /device:TPU:1, one launch (start us, length us, event | category | flops | bytes accessed | tf_op | source)
XLA Modules:
  0.0 79.1 jit_solution(9515954861411614391)
XLA Ops:
  0.0 0.0 copy-start
  0.0 0.0 copy-start.8
  0.0 3.2 %send_traces.1 = (bf16[16,16,256]{2,1,0:T(8,128)(2,1)S(1)}, bf16[16,16,256]{2,1,0:T(8,128)(2,1)}, bf16[16,64,256]{2,1,0:T(8,128)(2,1)S(1)}, bf16[96,16,256]{2,1,0:T(8,128)(2,1)S(1)}) custom-call(s32[1,2,16]{2,1,0:T(2,128)} %faces_ref.1, s32[1,2]{1,0:T(1,128)} %count_ref.1, bf16[16,64,256]{2,1,0:T(8,128)(2,1)} %dist_ref.1), custom_call_target="tpu_custom_call" | custom-call | tf_op jit(solution)/shard_map/send_traces/pallas_call | solution.py:330
  3.2 0.0 copy-start.2
  3.2 0.9 %copy-done.2 = bf16[96,16,256]{2,1,0:T(8,128)(2,1)} copy-done((bf16[96,16,256]{2,1,0:T(8,128)(2,1)}, bf16[96,16,256]{2,1,0:T(8,128)(2,1)S(1)}, u32[]{:S(2)}) %copy-start.2) | copy-done | bytes 786456
  4.1 0.0 copy-start.4
  4.1 0.8 %copy-done.4 = bf16[16,64,256]{2,1,0:T(8,128)(2,1)} copy-done((bf16[16,64,256]{2,1,0:T(8,128)(2,1)}, bf16[16,64,256]{2,1,0:T(8,128)(2,1)S(1)}, u32[]{:S(2)}) %copy-start.4) | copy-done | bytes 524312
  4.9 3.9 %collective-permute-start = (bf16[16,16,256]{2,1,0:T(8,128)(2,1)}, bf16[16,16,256]{2,1,0:T(8,128)(2,1)S(1)}, u32[]{:S(2)}, u32[]{:S(2)}) collective-permute-start(bf16[16,16,256]{2,1,0:T(8,128)(2,1)} %get-tuple-element.11), channel_id=1, source_target_pairs={{496,0},{0,16},{16,32},{32,48},{48,64},{64,80},{80,96},{96,112},{1... | collective-permute-start | bytes 393224 | tf_op jit(solution)/shard_map/ppermute | solution.py:24
  8.8 11.7 %collective-permute-start.1 = (bf16[16,16,256]{2,1,0:T(8,128)(2,1)S(1)}, bf16[16,16,256]{2,1,0:T(8,128)(2,1)S(1)}, u32[]{:S(2)}, u32[]{:S(2)}) collective-permute-start(bf16[16,16,256]{2,1,0:T(8,128)(2,1)S(1)} %get-tuple-element.12), channel_id=1, source_target_pairs={{16,0},{32,16},{48,32},{64,48},{80,64},{96,80},{112,96},{128,112},... | collective-permute-start | bytes 393224 | tf_op jit(solution)/shard_map/ppermute | solution.py:24
  20.5 0.0 copy-done
  20.5 0.0 copy-done.8
  20.5 0.0 copy-start.3
  20.5 1.1 %copy-done.3 = bf16[96,16,256]{2,1,0:T(8,128)(2,1)S(1)} copy-done((bf16[96,16,256]{2,1,0:T(8,128)(2,1)S(1)}, bf16[96,16,256]{2,1,0:T(8,128)(2,1)}, u32[]{:S(2)}) %copy-start.3) | copy-done | bytes 786456
  21.7 0.0 copy-start.5
  21.7 1.0 %copy-done.5 = bf16[16,64,256]{2,1,0:T(8,128)(2,1)S(1)} copy-done((bf16[16,64,256]{2,1,0:T(8,128)(2,1)S(1)}, bf16[16,64,256]{2,1,0:T(8,128)(2,1)}, u32[]{:S(2)}) %copy-start.5) | copy-done | bytes 524312
  22.7 1.8 %transport_local.1.part_ref = f32[16,64,256]{2,1,0:T(8,128)S(1)} custom-call(s32[6,16]{1,0:T(8,128)} %bitcast.7, s32[6,16]{1,0:T(8,128)} %bitcast.9, bf16[16,64,256]{2,1,0:T(8,128)(2,1)S(1)} %copy-done.5, bf16[96,16,256]{2,1,0:T(8,128)(2,1)S(1)} %copy-done.3, bf16[192,64]{1,0:T(8,128)(2,1)S(1)} %copy-done.8, bf16[6,5,64,128]{3,2,1,0:T(8,128)(2,1)S(1)} %copy-done), custom_call_target="tpu_custom_call" | custom-call | tf_op jit(solution)/shard_map/transport_local/pallas_call | solution.py:349
  24.5 0.0 collective-permute-done.prev_ref
  24.5 0.0 collective-permute-done.1.next_ref
  24.5 0.0 copy-start.1
  24.6 1.0 %copy-done.1 = bf16[6,5,64,128]{3,2,1,0:T(8,128)(2,1)S(1)} copy-done((bf16[6,5,64,128]{3,2,1,0:T(8,128)(2,1)S(1)}, bf16[6,5,64,128]{3,2,1,0:T(8,128)(2,1)}, u32[]{:S(2)}) %copy-start.1) | copy-done | bytes 491544
  25.6 2.2 %transport_remote.1 = bf16[16,64,256]{2,1,0:T(8,128)(2,1)} custom-call(s32[6,16]{1,0:T(8,128)} %bitcast.8, s32[6,16]{1,0:T(8,128)} %bitcast.10, f32[16,64,256]{2,1,0:T(8,128)S(1)} %transport_local.1.part_ref, bf16[16,16,256]{2,1,0:T(8,128)(2,1)S(1)} %collective-permute-done.prev_ref, bf16[16,16,256]{2,1,0:T(8,128)(2,1)S(1)} %collective-permute-done.1.next_ref, ...), custom_call_target="tpu_custom_call" | custom-call | tf_op jit(solution)/shard_map/transport_remote/pallas_call | solution.py:360
  27.8 0.0 copy-start.9
  27.8 0.0 copy-start.10
  27.8 8.2 %all-to-all-start = ((bf16[16,64,256]{2,1,0:T(8,128)(2,1)}), bf16[16,64,256]{2,1,0:T(8,128)(2,1)S(1)}, u32[]{:S(2)}, u32[]{:S(2)}) async-start(bf16[16,64,256]{2,1,0:T(8,128)(2,1)} %transport_remote.1), calls=%async_computation | async-start | bytes 1048576 | tf_op jit(solution)/shard_map/all_to_all | solution.py:380
  36.0 0.0 copy-done.9
  36.0 0.0 copy-done.10
  36.1 0.0 copy-start.11
  36.1 0.0 copy-start.7
  36.1 0.1 copy.13
  36.2 0.0 copy-start.6
  36.2 0.5 copy-done.11
  36.7 0.1 slice_multiply_fusion.kern_ref
  36.8 16.5 %all-to-all-done.dist_ref = bf16[16,64,256]{2,1,0:T(8,128)(2,1)S(1)} async-done(((bf16[16,64,256]{2,1,0:T(8,128)(2,1)}), bf16[16,64,256]{2,1,0:T(8,128)(2,1)S(1)}, u32[]{:S(2)}, u32[]{:S(2)}) %all-to-all-start) | async-done | bytes 524320 | tf_op jit(solution)/shard_map/all_to_all | solution.py:380
  53.3 0.0 copy-done.7
  53.3 0.0 copy-done.6
  53.3 4.9 %collide.1 = bf16[16,64,256]{2,1,0:T(8,128)(2,1)S(1)} custom-call(bf16[16,64,256]{2,1,0:T(8,128)(2,1)S(1)} %all-to-all-done.dist_ref, f32[9,16,256]{2,1,0:T(8,128)S(1)} %slice_multiply_fusion.kern_ref, bf16[2,256,256]{2,1,0:T(8,128)(2,1)S(1)} %copy-done.6, bf16[2,256,256]{2,1,0:T(8,128)(2,1)S(1)} %copy-done.7), custom_call_target="tpu_custom_call" | custom-call | tf_op jit(solution)/shard_map/collide/pallas_call | solution.py:382
  58.2 20.0 %all_to_all.10 = bf16[16,64,256]{2,1,0:T(8,128)(2,1)S(1)} all-to-all(bf16[16,64,256]{2,1,0:T(8,128)(2,1)S(1)} %collide.1), channel_id=1, replica_groups=mesh['space'=32,'vel'=16] {'vel'}, dimensions={0} | all-to-all | bytes 1048576 | tf_op jit(solution)/shard_map/all_to_all | solution.py:390
  78.3 0.8 %copy.15 = bf16[16,64,256]{2,1,0:T(8,128)(2,1)} copy(bf16[16,64,256]{2,1,0:T(8,128)(2,1)S(1)} %all_to_all.10) | data formatting | bytes 1048576
  (1 shorter events, 0.0 us)
Async XLA Ops:
  0.0 20.5 %copy-start = (bf16[6,5,64,128]{3,2,1,0:T(8,128)(2,1)S(1)}, bf16[6,5,64,128]{3,2,1,0:T(8,128)(2,1)}, u32[]{:S(2)}) copy-start(bf16[6,5,64,128]{3,2,1,0:T(8,128)(2,1)} %constant.10.clone.lift_ref) | copy-start | bytes 1474564
  0.0 20.5 %copy-start.8 = (bf16[192,64]{1,0:T(8,128)(2,1)S(1)}, bf16[192,64]{1,0:T(8,128)(2,1)}, u32[]{:S(2)}) copy-start(bf16[192,64]{1,0:T(8,128)(2,1)} %constant.11.clone.gradient_ref) | copy-start | bytes 73732
  3.2 0.9 %copy-start.2 = (bf16[96,16,256]{2,1,0:T(8,128)(2,1)}, bf16[96,16,256]{2,1,0:T(8,128)(2,1)S(1)}, u32[]{:S(2)}) copy-start(bf16[96,16,256]{2,1,0:T(8,128)(2,1)S(1)} %get-tuple-element.10.rows) | copy-start | bytes 2359300
  4.1 0.8 %copy-start.4 = (bf16[16,64,256]{2,1,0:T(8,128)(2,1)}, bf16[16,64,256]{2,1,0:T(8,128)(2,1)S(1)}, u32[]{:S(2)}) copy-start(bf16[16,64,256]{2,1,0:T(8,128)(2,1)S(1)} %get-tuple-element.9.held) | copy-start | bytes 1572868
  4.9 19.6 %collective-permute-start = (bf16[16,16,256]{2,1,0:T(8,128)(2,1)}, bf16[16,16,256]{2,1,0:T(8,128)(2,1)S(1)}, u32[]{:S(2)}, u32[]{:S(2)}) collective-permute-start(bf16[16,16,256]{2,1,0:T(8,128)(2,1)} %get-tuple-element.11), channel_id=1, source_target_pairs={{496,0},{0,16},{16,32},{32,48},{48,64},{64,80},{80,96},{96,112},{1... | collective-permute-start | bytes 393224 | tf_op jit(solution)/shard_map/ppermute | solution.py:24
  8.8 15.7 %collective-permute-start.1 = (bf16[16,16,256]{2,1,0:T(8,128)(2,1)S(1)}, bf16[16,16,256]{2,1,0:T(8,128)(2,1)S(1)}, u32[]{:S(2)}, u32[]{:S(2)}) collective-permute-start(bf16[16,16,256]{2,1,0:T(8,128)(2,1)S(1)} %get-tuple-element.12), channel_id=1, source_target_pairs={{16,0},{32,16},{48,32},{64,48},{80,64},{96,80},{112,96},{128,112},... | collective-permute-start | bytes 393224 | tf_op jit(solution)/shard_map/ppermute | solution.py:24
  20.5 1.1 %copy-start.3 = (bf16[96,16,256]{2,1,0:T(8,128)(2,1)S(1)}, bf16[96,16,256]{2,1,0:T(8,128)(2,1)}, u32[]{:S(2)}) copy-start(bf16[96,16,256]{2,1,0:T(8,128)(2,1)} %copy-done.2) | copy-start | bytes 2359300
  21.7 1.0 %copy-start.5 = (bf16[16,64,256]{2,1,0:T(8,128)(2,1)S(1)}, bf16[16,64,256]{2,1,0:T(8,128)(2,1)}, u32[]{:S(2)}) copy-start(bf16[16,64,256]{2,1,0:T(8,128)(2,1)} %copy-done.4) | copy-start | bytes 1572868
  24.5 1.0 %copy-start.1 = (bf16[6,5,64,128]{3,2,1,0:T(8,128)(2,1)S(1)}, bf16[6,5,64,128]{3,2,1,0:T(8,128)(2,1)}, u32[]{:S(2)}) copy-start(bf16[6,5,64,128]{3,2,1,0:T(8,128)(2,1)} %constant.10.clone.lift_ref) | copy-start | bytes 1474564
  27.8 8.2 %copy-start.9 = (f32[5,4096]{1,0:T(8,128)S(1)}, f32[5,4096]{1,0:T(8,128)}, u32[]{:S(2)}) copy-start(f32[5,4096]{1,0:T(8,128)} %param.18) | copy-start | bytes 245764
  27.8 8.2 %copy-start.10 = (f32[4,4096]{1,0:T(4,128)S(1)}, f32[4,4096]{1,0:T(4,128)}, u32[]{:S(2)}) copy-start(f32[4,4096]{1,0:T(4,128)} %param.17) | copy-start | bytes 196612
  27.8 25.5 %all-to-all-start = ((bf16[16,64,256]{2,1,0:T(8,128)(2,1)}), bf16[16,64,256]{2,1,0:T(8,128)(2,1)S(1)}, u32[]{:S(2)}, u32[]{:S(2)}) async-start(bf16[16,64,256]{2,1,0:T(8,128)(2,1)} %transport_remote.1), calls=%async_computation | async-start | bytes 1048576 | tf_op jit(solution)/shard_map/all_to_all | solution.py:380
  36.1 0.7 copy-start.11
  36.1 17.2 %copy-start.7 = (bf16[2,256,256]{2,1,0:T(8,128)(2,1)S(1)}, bf16[2,256,256]{2,1,0:T(8,128)(2,1)}, u32[]{:S(2)}) copy-start(bf16[2,256,256]{2,1,0:T(8,128)(2,1)} %constant.13.clone.back_ref) | copy-start | bytes 786436
  36.2 17.1 %copy-start.6 = (bf16[2,256,256]{2,1,0:T(8,128)(2,1)S(1)}, bf16[2,256,256]{2,1,0:T(8,128)(2,1)}, u32[]{:S(2)}) copy-start(bf16[2,256,256]{2,1,0:T(8,128)(2,1)} %constant.12.clone.into_ref) | copy-start | bytes 786436

commit v3 on v2

--- a/solution.py
+++ b/solution.py
@@ -10,7 +10,7 @@
 VSIDE = 16
 SLOTS = 16
 GROUP = 16
-PIECES = 4
+SCOPED = 16 << 20
 
 
 courant = 0.1
@@ -177,54 +177,65 @@
     return [one.astype(jnp.bfloat16) for one in ones]
 
 
-def send_kernel(faces_ref, count_ref, dist_ref, back_ref, ahead_ref, held, rows, sems):
+def fetched(sems, *pairs):
+    copies = [pltpu.make_async_copy(src, dst, sems.at[i]) for i, (src, dst) in enumerate(pairs)]
+    for copy in copies:
+        copy.start()
+    return copies
+
+
+def face_selector(nodes):
+    node = lax.broadcasted_iota(jnp.int32, (16, nodes), 1)
+    picks = [jnp.where(face_nodes(f, (16, nodes), 0) == node, 1.0, 0.0) for f in range(6)]
+    return jnp.concatenate(picks, axis=0).astype(jnp.bfloat16)
+
+
+def extract_traces(held, rows):
     elements, nodes, width = held.shape
-    step = elements // PIECES
-
-    def piece(at):
-        part = pl.ds(at * step, step)
-        return pltpu.make_async_copy(dist_ref.at[part], held.at[part], sems.at[at])
-
-    for at in range(PIECES):
-        piece(at).start()
-    node = lax.broadcasted_iota(jnp.int32, (16, nodes), 1)
-    select = jnp.concatenate(
-        [jnp.where(face_nodes(f, (16, nodes), 0) == node, 1.0, 0.0) for f in range(6)], axis=0
-    ).astype(jnp.bfloat16)
+    select = face_selector(nodes)
     for at in range(elements):
-        if at % step == 0:
-            piece(at // step).wait()
         traces = dot(select, held[at]).astype(jnp.bfloat16)
         rows[6 * at : 6 * at + 6] = traces.reshape(6, 16, width)
+
+
+def send_kernel(faces_hbm, count_hbm, dist_hbm, back_ref, ahead_ref, held, rows, faces, count, sems):
+    copies = fetched(sems, (faces_hbm, faces), (count_hbm, count), (dist_hbm, held))
+    for copy in copies:
+        copy.wait()
+    extract_traces(held, rows)
     for way, out in enumerate((back_ref, ahead_ref)):
         for slot in range(SLOTS):
-            trace = rows[faces_ref[0, way, slot]]
-            keep = jnp.where(slot < count_ref[0, way], 1.0, 0.0).astype(jnp.bfloat16)
-            out[slot] = trace * keep
-
-
-def lift_traces(at, level_ref, lift_ref, stack, total):
+            keep = jnp.where(slot < count[0, way], 1.0, 0.0).astype(jnp.bfloat16)
+            out[slot] = rows[faces[0, way, slot]] * keep
+
+
+def add_lifts(left, stacked, total):
     speeds = local_speeds((1, total.shape[-1]))
-    left = jnp.concatenate(
-        [
-            lift_ref[2 * axis, level_ref[2 * axis, at]]
-            + lift_ref[2 * axis + 1, level_ref[2 * axis + 1, at]]
-            for axis in range(3)
-        ],
-        axis=0,
-    )
-    lifted = dot(left, stack[at])
+    lifted = dot(left, stacked)
     for axis in range(3):
         weight = -courant * lift_weight * speeds[axis]
         total = total + lifted[64 * axis : 64 * axis + 64] * weight
     return total
 
 
-def local_kernel(source_ref, level_ref, held, rows, gradient_ref, lift_ref, out_ref, table, stack):
+def local_kernel(
+    source_hbm,
+    level_hbm,
+    dist_hbm,
+    gradient_ref,
+    lift_ref,
+    out_ref,
+    left_ref,
+    held,
+    rows,
+    stack,
+    source,
+    level,
+    sems,
+):
+    copies = fetched(sems, (source_hbm, source), (level_hbm, level), (dist_hbm, held))
     elements, nodes, width = held.shape
     faces = 6 * elements
-    table[:faces] = rows[...]
-    table[faces] = jnp.zeros((16, width), jnp.bfloat16)
     speeds = local_speeds((1, width))
     masks = inflow_masks((16, width))
     wide = local_speeds((nodes, width))
@@ -235,37 +246,55 @@
         member = jnp.logical_and(on, digits[face // 2] == 3 * (face % 2))
         loss = loss + jnp.where(member, jnp.abs(wide[face // 2]), 0.0)
     keep = 1.0 - courant * lift_weight * loss
+    for copy in copies:
+        copy.wait()
+    extract_traces(held, rows)
+    rows[faces] = jnp.zeros((16, width), jnp.bfloat16)
     for at in range(elements):
         for face in range(6):
-            trace = table[jnp.minimum(source_ref[face, at], faces)] * masks[face]
+            trace = rows[jnp.minimum(source[face, at], faces)] * masks[face]
             stack[at, 16 * face : 16 * face + 16] = trace
         stack[at, 96:] = jnp.zeros((32, width), jnp.bfloat16)
         total = held[at].astype(jnp.float32) * keep
         moved = dot(gradient_ref[...], held[at])
         for axis in range(3):
             total = total + moved[64 * axis : 64 * axis + 64] * (-courant * speeds[axis])
-        out_ref[at] = lift_traces(at, level_ref, lift_ref, stack, total)
-
-
-def remote_kernel(source_ref, level_ref, part_ref, prev_ref, next_ref, lift_ref, out_ref, table, stack):
+        left = jnp.concatenate(
+            [
+                lift_ref[2 * axis, level[2 * axis, at]] + lift_ref[2 * axis + 1, level[2 * axis + 1, at]]
+                for axis in range(3)
+            ],
+            axis=0,
+        )
+        left_ref[at] = left
+        out_ref[at] = add_lifts(left, stack[at], total)
+
+
+def remote_kernel(
+    source_hbm, part_ref, left_ref, prev_ref, next_ref, out_ref, table, stack, source, sems
+):
+    copies = fetched(sems, (source_hbm, source))
     elements, _, width = part_ref.shape
     faces = 6 * elements
     table[0] = jnp.zeros((16, width), jnp.bfloat16)
     table[1 : SLOTS + 1] = prev_ref[...]
     table[SLOTS + 1 :] = next_ref[...]
     masks = inflow_masks((16, width))
+    for copy in copies:
+        copy.wait()
     for at in range(elements):
         for face in range(6):
-            trace = table[jnp.maximum(source_ref[face, at] - (faces - 1), 0)] * masks[face]
+            trace = table[jnp.maximum(source[face, at] - (faces - 1), 0)] * masks[face]
             stack[at, 16 * face : 16 * face + 16] = trace
         stack[at, 96:] = jnp.zeros((32, width), jnp.bfloat16)
-        total = lift_traces(at, level_ref, lift_ref, stack, part_ref[at])
-        out_ref[at] = total.astype(jnp.bfloat16)
-
-
-def collide_kernel(dist_ref, kern_ref, into_ref, back_ref, out_ref, spectrum, fields, first, gain):
+        out_ref[at] = add_lifts(left_ref[at], stack[at], part_ref[at]).astype(jnp.bfloat16)
+
+
+def collide_kernel(
+    dist_ref, alpha_ref, beta_ref, into_ref, back_ref, out_ref, spectrum, fields, first, gain
+):
     nodes, plane = dist_ref.shape[1], dist_ref.shape[2]
-    modes = (kern_ref.shape[0] - 1) // 2
+    modes = alpha_ref.shape[0]
     order = [m for pair in range(modes) for m in (pair, modes + pair)] + [2 * modes]
     halves = [slice(0, plane // 2), slice(plane // 2, plane)]
 
@@ -278,11 +307,13 @@
         fields[0] = dot(values, into_ref[0]) + dot(values, into_ref[1])
         for lanes in halves:
             for i, part in enumerate(cosine_forward(planes(0, lanes))):
-                spectrum[i, :, lanes] = part
+                spectrum[i, :, lanes] = part if i else 0.5 * part
 
         def filtered(which, slot):
+            kern = alpha_ref if which < modes else beta_ref
+            row = which % modes if which < 2 * modes else modes
             parts = [
-                (spectrum[i] * kern_ref[which, i : i + 1, :]).astype(jnp.bfloat16)
+                (spectrum[i] * kern[row : row + 1, i * plane : (i + 1) * plane]).astype(jnp.bfloat16)
                 for i in range(VSIDE)
             ]
             left = jnp.concatenate(parts, axis=0)
@@ -313,12 +344,16 @@
     return pl.BlockSpec(memory_space=pltpu.VMEM)
 
 
-def in_smem():
-    return pl.BlockSpec(memory_space=pltpu.SMEM)
+def in_hbm():
+    return pl.BlockSpec(memory_space=pltpu.HBM)
 
 
 def on_chip(array):
     return pltpu.with_memory_space_constraint(array, pltpu.VMEM)
+
+
+def off_chip(*arrays):
+    return [pltpu.with_memory_space_constraint(array, pltpu.HBM) for array in arrays]
 
 
 def on_device(dist, send_faces, send_count, source_face, subface, alpha, beta):
@@ -326,67 +361,80 @@
     faces = 6 * elements
     gradients, _, _ = static_tables()
     traces = pltpu.VMEM((SLOTS, 16, width), jnp.bfloat16)
-
-    back, ahead, held, rows = pl.pallas_call(
+    block = pltpu.VMEM(dist.shape, jnp.bfloat16)
+
+    back, ahead = pl.pallas_call(
         send_kernel,
-        out_shape=(
-            traces,
-            traces,
-            pltpu.VMEM(dist.shape, jnp.bfloat16),
+        out_shape=(traces, traces),
+        in_specs=[in_hbm()] * 3,
+        out_specs=(in_vmem(), in_vmem()),
+        scratch_shapes=[
+            block,
             pltpu.VMEM((faces, 16, width), jnp.bfloat16),
-        ),
-        in_specs=[in_smem(), in_smem(), pl.BlockSpec(memory_space=pl.ANY)],
-        out_specs=(in_vmem(),) * 4,
-        scratch_shapes=[pltpu.SemaphoreType.DMA((PIECES,))],
+            pltpu.SMEM(send_faces.shape, jnp.int32),
+            pltpu.SMEM(send_count.shape, jnp.int32),
+            pltpu.SemaphoreType.DMA((3,)),
+        ],
+        compiler_params=pltpu.CompilerParams(vmem_limit_bytes=SCOPED),
         name="send_traces",
-    )(send_faces, send_count, dist)
+    )(*off_chip(send_faces, send_count, dist))
     from_prev = passed_along(ahead, "space", 1)
     from_next = passed_along(back, "space", -1)
 
     sources, levels = source_face.T, subface.T
-    lifts = on_chip(jnp.asarray(mortar_lifts()))
-    gradient = on_chip(jnp.asarray(gradients.reshape(3 * nodes, nodes), jnp.bfloat16))
-    part = pl.pallas_call(
+    lifts = jnp.asarray(mortar_lifts())
+    gradient = jnp.asarray(gradients.reshape(3 * nodes, nodes), jnp.bfloat16)
+    indices = pltpu.SMEM(sources.shape, jnp.int32)
+    part, left = pl.pallas_call(
         local_kernel,
-        out_shape=pltpu.VMEM(dist.shape, jnp.float32),
-        in_specs=[in_smem(), in_smem()] + [in_vmem()] * 4,
-        out_specs=in_vmem(),
+        out_shape=(
+            pltpu.VMEM(dist.shape, jnp.float32),
+            pltpu.VMEM((elements, 3 * nodes, 128), jnp.bfloat16),
+        ),
+        in_specs=[in_hbm()] * 3 + [in_vmem()] * 2,
+        out_specs=(in_vmem(), in_vmem()),
         scratch_shapes=[
+            block,
             pltpu.VMEM((faces + 1, 16, width), jnp.bfloat16),
             pltpu.VMEM((elements, 128, width), jnp.bfloat16),
+            indices,
+            indices,
+            pltpu.SemaphoreType.DMA((3,)),
         ],
+        compiler_params=pltpu.CompilerParams(vmem_limit_bytes=SCOPED),
         name="transport_local",
-    )(sources, levels, on_chip(held), on_chip(rows), gradient, lifts)
+    )(*off_chip(sources, levels, dist), on_chip(gradient), on_chip(lifts))
     updated = pl.pallas_call(
         remote_kernel,
-        out_shape=pltpu.VMEM(dist.shape, jnp.bfloat16),
-        in_specs=[in_smem(), in_smem()] + [in_vmem()] * 4,
+        out_shape=block,
+        in_specs=[in_hbm()] + [in_vmem()] * 4,
         out_specs=in_vmem(),
         scratch_shapes=[
             pltpu.VMEM((2 * SLOTS + 1, 16, width), jnp.bfloat16),
             pltpu.VMEM((elements, 128, width), jnp.bfloat16),
+            indices,
+            pltpu.SemaphoreType.DMA((1,)),
         ],
+        compiler_params=pltpu.CompilerParams(vmem_limit_bytes=SCOPED),
         name="transport_remote",
-    )(sources, levels, on_chip(part), on_chip(from_prev), on_chip(from_next), lifts)
+    )(*off_chip(sources), on_chip(part), on_chip(left), on_chip(from_prev), on_chip(from_next))
 
     plane = VSIDE * VSIDE
     cosine = cosine_table()
     pair = np.kron(cosine, cosine)
-    into = on_chip(jnp.asarray(np.stack(split_table(pair.T))))
-    out_of = on_chip(jnp.asarray(np.stack(split_table(pair))))
-    norms = np.full((VSIDE, 1), 2.0 / VSIDE, np.float32)
-    norms[0] = 1.0 / VSIDE
-    kernels = jnp.concatenate([alpha, beta], axis=0).reshape(-1, VSIDE, plane) * norms
+    into = jnp.asarray(np.stack(split_table(pair.T * (2.0 / VSIDE))))
+    out_of = jnp.asarray(np.stack(split_table(pair)))
     whole = lax.all_to_all(updated, "vel", split_axis=0, concat_axis=0, tiled=True)
     cube = pltpu.VMEM((VSIDE, GROUP, plane), jnp.float32)
     mixed = pl.pallas_call(
         collide_kernel,
         out_shape=pltpu.VMEM(whole.shape, jnp.bfloat16),
-        in_specs=[in_vmem()] * 4,
+        in_specs=[in_vmem()] * 5,
         out_specs=in_vmem(),
         scratch_shapes=[cube, pltpu.VMEM((2, VSIDE * GROUP, plane), jnp.float32), cube, cube],
+        compiler_params=pltpu.CompilerParams(vmem_limit_bytes=SCOPED),
         name="collide",
-    )(on_chip(whole), on_chip(kernels), into, out_of)
+    )(*[on_chip(array) for array in (whole, alpha, beta, into, out_of)])
     return lax.all_to_all(mixed, "vel", split_axis=0, concat_axis=0, tiled=True)
 
 

time: 79.6 us -> 73.2 us (0.920)
  blocking collectives: 20 us -> 45.3 us
  waiting for transfers between devices: 16.5 us -> 0.01 us
  starting transfers between devices: 23.8 us -> 15.6 us
  local copies, waits for them, and re-layouts: 6.32 us -> 1.62 us
  Pallas kernels: 12.1 us -> 10.2 us
    all_to_all x0 -> x1, blocking collectives: none -> 25.3 us  [on_device(): lax.all_to_all(updated, 'vel', split_axis=0, concat_axis=0, tiled=True)]
    all_to_all x1 -> x0, waiting for transfers between devices: 16.5 us -> none  [on_device(): lax.all_to_all(updated, 'vel', split_axis=0, concat_axis=0, tiled=True)]
    all_to_all x1 -> x0, starting transfers between devices: 8.2 us -> none  [on_device(): lax.all_to_all(updated, 'vel', split_axis=0, concat_axis=0, tiled=True)]
    unnamed x26 -> x13, local copies, waits for them, and re-layouts: 6.32 us -> 1.62 us
    pallas_call x3, Pallas kernels: 7.22 us -> 5.28 us  [the longest x1 2.44 us: on_device(): pl.pallas_call(local_kernel, out_shape=(pltpu.VMEM(dist.shape, jnp.float3...]
  transfers between devices with their start and end apart: 3 -> 2, of which waited for: 1 -> 0; matrix products, arithmetic and copies ran while one was open for 0% -> 0% of each run, Pallas kernels for 2% -> 3%
where the time goes in v3:
time: 73.2 us; the launch traced here: 72.9 us
  blocking collectives  45.3 us (62%)
  starting transfers between devices  15.6 us (21%)
  Pallas kernels  10.2 us (14%)
  local copies, waits for them, and re-layouts  1.62 us (2%)
    all_to_all x1, blocking collectives, on_device(): lax.all_to_all(updated, 'vel', split_axis=0, concat_axis=0, tiled=True)  25.3 us
    all_to_all x1, blocking collectives, on_device(): return lax.all_to_all(mixed, 'vel', split_axis=0, concat_axis=0, tiled=True)  20 us
    ppermute x2, starting transfers between devices, passed_along(): return lax.ppermute(block, axis, route)  15.6 us
    pallas_call x1, Pallas kernels, on_device(): pl.pallas_call(collide_kernel, out_shape=pltpu.VMEM(whole.shape, jnp.bflo...  4.91 us
    pallas_call x1, Pallas kernels, on_device(): pl.pallas_call(local_kernel, out_shape=(pltpu.VMEM(dist.shape, jnp.float3...  2.44 us
    unnamed x13, local copies, waits for them, and re-layouts  1.62 us
    pallas_call x1, Pallas kernels, on_device(): pl.pallas_call(send_kernel, out_shape=(traces, traces), in_specs=[in_hbm(...  1.54 us
  transfers between devices with their start and end apart: 2, of which 0 were waited for; matrix products, arithmetic and copies ran while one was open for 0% of the time, Pallas kernels for 3%

profile of v3, /device:TPU:1, one launch (start us, length us, event | category | flops | bytes accessed | tf_op | source)
XLA Modules:
  0.0 72.9 jit_solution(2022621223451997279)
XLA Ops:
  0.0 0.0 copy-start
  0.0 1.5 %send_traces.1 = (bf16[16,16,256]{2,1,0:T(8,128)(2,1)S(1)}, bf16[16,16,256]{2,1,0:T(8,128)(2,1)S(1)}) custom-call(s32[1,2,16]{2,1,0:T(2,128)} %faces_hbm.1, s32[1,2]{1,0:T(1,128)} %count_hbm.1, bf16[16,64,256]{2,1,0:T(8,128)(2,1)} %dist_hbm.3), custom_call_target="tpu_custom_call" | custom-call | tf_op jit(solution)/shard_map/send_traces/pallas_call | solution.py:366
  1.5 3.9 %collective-permute-start = (bf16[16,16,256]{2,1,0:T(8,128)(2,1)S(1)}, bf16[16,16,256]{2,1,0:T(8,128)(2,1)S(1)}, u32[]{:S(2)}, u32[]{:S(2)}) collective-permute-start(bf16[16,16,256]{2,1,0:T(8,128)(2,1)S(1)} %get-tuple-element.11), channel_id=1, source_target_pairs={{496,0},{0,16},{16,32},{32,48},{48,64},{64,80},{80,96},{96,112},{1... | collective-permute-start | bytes 393224 | tf_op jit(solution)/shard_map/ppermute | solution.py:24
  5.5 11.7 %collective-permute-start.1 = (bf16[16,16,256]{2,1,0:T(8,128)(2,1)S(1)}, bf16[16,16,256]{2,1,0:T(8,128)(2,1)S(1)}, u32[]{:S(2)}, u32[]{:S(2)}) collective-permute-start(bf16[16,16,256]{2,1,0:T(8,128)(2,1)S(1)} %get-tuple-element.12), channel_id=1, source_target_pairs={{16,0},{32,16},{48,32},{64,48},{80,64},{96,80},{112,96},{128,112},... | collective-permute-start | bytes 393224 | tf_op jit(solution)/shard_map/ppermute | solution.py:24
  17.2 0.0 copy-done
  17.2 0.0 copy-start.5
  17.2 0.8 %copy-done.5 = bf16[192,64]{1,0:T(8,128)(2,1)S(1)} copy-done((bf16[192,64]{1,0:T(8,128)(2,1)S(1)}, bf16[192,64]{1,0:T(8,128)(2,1)}, u32[]{:S(2)}) %copy-start.5) | copy-done | bytes 24600
  18.0 2.4 %transport_local.1 = (f32[16,64,256]{2,1,0:T(8,128)S(1)}, bf16[16,192,128]{2,1,0:T(8,128)(2,1)S(1)}) custom-call(s32[6,16]{1,0:T(8,128)} %bitcast.2, s32[6,16]{1,0:T(8,128)} %bitcast.4, bf16[16,64,256]{2,1,0:T(8,128)(2,1)} %dist_hbm.3, bf16[192,64]{1,0:T(8,128)(2,1)S(1)} %copy-done.5, bf16[6,5,64,128]{3,2,1,0:T(8,128)(2,1)S(1)} %copy-done), custom_call_target="tpu_custom_call" | custom-call | tf_op jit(solution)/shard_map/transport_local/pallas_call | solution.py:388
  20.4 0.0 collective-permute-done.prev_ref
  20.4 0.0 collective-permute-done.1.next_ref
  20.5 1.3 %transport_remote.1 = bf16[16,64,256]{2,1,0:T(8,128)(2,1)S(1)} custom-call(s32[6,16]{1,0:T(8,128)} %bitcast.3, f32[16,64,256]{2,1,0:T(8,128)S(1)} %get-tuple-element.9.part_ref, bf16[16,192,128]{2,1,0:T(8,128)(2,1)S(1)} %get-tuple-element.10.left_ref, bf16[16,16,256]{2,1,0:T(8,128)(2,1)S(1)} %collective-permute-done.prev_ref, ...), custom_call_target="tpu_custom_call" | custom-call | tf_op jit(solution)/shard_map/transport_remote/pallas_call | solution.py:407
  21.8 0.0 copy-start.1
  21.8 0.0 copy-start.2
  21.8 0.0 copy-start.3
  21.8 0.0 copy-start.4
  21.8 25.3 %all_to_all.10.dist_ref = bf16[16,64,256]{2,1,0:T(8,128)(2,1)S(1)} all-to-all(bf16[16,64,256]{2,1,0:T(8,128)(2,1)S(1)} %transport_remote.1), channel_id=1, replica_groups=mesh['space'=32,'vel'=16] {'vel'}, dimensions={0} | all-to-all | bytes 1048576 | tf_op jit(solution)/shard_map/all_to_all | solution.py:427
  47.1 0.0 copy-done.1
  47.1 0.0 copy-done.2
  47.1 0.0 copy-done.3
  47.1 0.0 copy-done.4
  47.2 4.9 %collide.1 = bf16[16,64,256]{2,1,0:T(8,128)(2,1)S(1)} custom-call(bf16[16,64,256]{2,1,0:T(8,128)(2,1)S(1)} %all_to_all.10.dist_ref, f32[4,4096]{1,0:T(4,128)S(1)} %copy-done.4, f32[5,4096]{1,0:T(8,128)S(1)} %copy-done.3, bf16[2,256,256]{2,1,0:T(8,128)(2,1)S(1)} %copy-done.2, bf16[2,256,256]{2,1,0:T(8,128)(2,1)S(1)} %copy-done.1), custom_call_target="tpu_custom_call" | custom-call | tf_op jit(solution)/shard_map/collide/pallas_call | solution.py:429
  52.1 20.0 %all_to_all.11 = bf16[16,64,256]{2,1,0:T(8,128)(2,1)S(1)} all-to-all(bf16[16,64,256]{2,1,0:T(8,128)(2,1)S(1)} %collide.1), channel_id=1, replica_groups=mesh['space'=32,'vel'=16] {'vel'}, dimensions={0} | all-to-all | bytes 1048576 | tf_op jit(solution)/shard_map/all_to_all | solution.py:438
  72.1 0.8 %copy.13 = bf16[16,64,256]{2,1,0:T(8,128)(2,1)} copy(bf16[16,64,256]{2,1,0:T(8,128)(2,1)S(1)} %all_to_all.11) | data formatting | bytes 1048576
Async XLA Ops:
  0.0 17.2 %copy-start = (bf16[6,5,64,128]{3,2,1,0:T(8,128)(2,1)S(1)}, bf16[6,5,64,128]{3,2,1,0:T(8,128)(2,1)}, u32[]{:S(2)}) copy-start(bf16[6,5,64,128]{3,2,1,0:T(8,128)(2,1)} %constant.8.clone.lift_ref) | copy-start | bytes 1474564
  1.5 18.9 %collective-permute-start = (bf16[16,16,256]{2,1,0:T(8,128)(2,1)S(1)}, bf16[16,16,256]{2,1,0:T(8,128)(2,1)S(1)}, u32[]{:S(2)}, u32[]{:S(2)}) collective-permute-start(bf16[16,16,256]{2,1,0:T(8,128)(2,1)S(1)} %get-tuple-element.11), channel_id=1, source_target_pairs={{496,0},{0,16},{16,32},{32,48},{48,64},{64,80},{80,96},{96,112},{1... | collective-permute-start | bytes 393224 | tf_op jit(solution)/shard_map/ppermute | solution.py:24
  5.5 14.9 %collective-permute-start.1 = (bf16[16,16,256]{2,1,0:T(8,128)(2,1)S(1)}, bf16[16,16,256]{2,1,0:T(8,128)(2,1)S(1)}, u32[]{:S(2)}, u32[]{:S(2)}) collective-permute-start(bf16[16,16,256]{2,1,0:T(8,128)(2,1)S(1)} %get-tuple-element.12), channel_id=1, source_target_pairs={{16,0},{32,16},{48,32},{64,48},{80,64},{96,80},{112,96},{128,112},... | collective-permute-start | bytes 393224 | tf_op jit(solution)/shard_map/ppermute | solution.py:24
  17.2 0.8 %copy-start.5 = (bf16[192,64]{1,0:T(8,128)(2,1)S(1)}, bf16[192,64]{1,0:T(8,128)(2,1)}, u32[]{:S(2)}) copy-start(bf16[192,64]{1,0:T(8,128)(2,1)} %constant.9.clone.gradient_ref) | copy-start | bytes 73732
  21.8 25.4 %copy-start.1 = (bf16[2,256,256]{2,1,0:T(8,128)(2,1)S(1)}, bf16[2,256,256]{2,1,0:T(8,128)(2,1)}, u32[]{:S(2)}) copy-start(bf16[2,256,256]{2,1,0:T(8,128)(2,1)} %constant.11.clone.back_ref) | copy-start | bytes 786436
  21.8 25.4 %copy-start.2 = (bf16[2,256,256]{2,1,0:T(8,128)(2,1)S(1)}, bf16[2,256,256]{2,1,0:T(8,128)(2,1)}, u32[]{:S(2)}) copy-start(bf16[2,256,256]{2,1,0:T(8,128)(2,1)} %constant.10.clone.into_ref) | copy-start | bytes 786436
  21.8 25.3 %copy-start.3 = (f32[5,4096]{1,0:T(8,128)S(1)}, f32[5,4096]{1,0:T(8,128)}, u32[]{:S(2)}) copy-start(f32[5,4096]{1,0:T(8,128)} %beta_ref.1) | copy-start | bytes 245764
  21.8 25.3 %copy-start.4 = (f32[4,4096]{1,0:T(4,128)S(1)}, f32[4,4096]{1,0:T(4,128)}, u32[]{:S(2)}) copy-start(f32[4,4096]{1,0:T(4,128)} %alpha_ref.1) | copy-start | bytes 196612

commit v4 on v3

--- a/solution.py
+++ b/solution.py
@@ -106,14 +106,16 @@
     return (high, np.asarray(rest, np.float32).astype(ml_dtypes.bfloat16))
 
 
-def mortar_lifts():
-    _, selector, mortar = static_tables()
-    tables = np.zeros((6, 5, 64, 128))
+def transport_tables():
+    gradients, selector, mortar = static_tables()
+    tables = np.zeros((33, 64, 128))
     for face in range(6):
         lift = selector[face * 16 : face * 16 + 16].T
         sign = -1.0 if face % 2 == 0 else 1.0
         for level in range(5):
-            tables[face, level, :, face * 16 : face * 16 + 16] = sign * (lift @ mortar[level])
+            placed = sign * (lift @ mortar[level])
+            tables[5 * face + level, :, face * 16 : face * 16 + 16] = placed
+    tables[30:, :, :64] = gradients
     return tables.astype(np.float32).astype(ml_dtypes.bfloat16)
 
 
@@ -203,6 +205,7 @@
     for copy in copies:
         copy.wait()
     extract_traces(held, rows)
+    rows[6 * held.shape[0]] = jnp.zeros(rows.shape[1:], jnp.bfloat16)
     for way, out in enumerate((back_ref, ahead_ref)):
         for slot in range(SLOTS):
             keep = jnp.where(slot < count[0, way], 1.0, 0.0).astype(jnp.bfloat16)
@@ -219,21 +222,9 @@
 
 
 def local_kernel(
-    source_hbm,
-    level_hbm,
-    dist_hbm,
-    gradient_ref,
-    lift_ref,
-    out_ref,
-    left_ref,
-    held,
-    rows,
-    stack,
-    source,
-    level,
-    sems,
+    source_hbm, level_hbm, held, rows, table_ref, out_ref, left_ref, stack, source, level, sems
 ):
-    copies = fetched(sems, (source_hbm, source), (level_hbm, level), (dist_hbm, held))
+    copies = fetched(sems, (source_hbm, source), (level_hbm, level))
     elements, nodes, width = held.shape
     faces = 6 * elements
     speeds = local_speeds((1, width))
@@ -248,20 +239,20 @@
     keep = 1.0 - courant * lift_weight * loss
     for copy in copies:
         copy.wait()
-    extract_traces(held, rows)
-    rows[faces] = jnp.zeros((16, width), jnp.bfloat16)
+    gradient = table_ref[30:].reshape(3 * nodes, table_ref.shape[2])[:, :nodes]
     for at in range(elements):
         for face in range(6):
             trace = rows[jnp.minimum(source[face, at], faces)] * masks[face]
             stack[at, 16 * face : 16 * face + 16] = trace
         stack[at, 96:] = jnp.zeros((32, width), jnp.bfloat16)
         total = held[at].astype(jnp.float32) * keep
-        moved = dot(gradient_ref[...], held[at])
+        moved = dot(gradient, held[at])
         for axis in range(3):
             total = total + moved[64 * axis : 64 * axis + 64] * (-courant * speeds[axis])
         left = jnp.concatenate(
             [
-                lift_ref[2 * axis, level[2 * axis, at]] + lift_ref[2 * axis + 1, level[2 * axis + 1, at]]
+                table_ref[10 * axis + level[2 * axis, at]]
+                + table_ref[10 * axis + 5 + level[2 * axis + 1, at]]
                 for axis in range(3)
             ],
             axis=0,
@@ -359,18 +350,15 @@
 def on_device(dist, send_faces, send_count, source_face, subface, alpha, beta):
     elements, nodes, width = dist.shape
     faces = 6 * elements
-    gradients, _, _ = static_tables()
     traces = pltpu.VMEM((SLOTS, 16, width), jnp.bfloat16)
     block = pltpu.VMEM(dist.shape, jnp.bfloat16)
 
-    back, ahead = pl.pallas_call(
+    back, ahead, held, rows = pl.pallas_call(
         send_kernel,
-        out_shape=(traces, traces),
+        out_shape=(traces, traces, block, pltpu.VMEM((faces + 1, 16, width), jnp.bfloat16)),
         in_specs=[in_hbm()] * 3,
-        out_specs=(in_vmem(), in_vmem()),
+        out_specs=(in_vmem(),) * 4,
         scratch_shapes=[
-            block,
-            pltpu.VMEM((faces, 16, width), jnp.bfloat16),
             pltpu.SMEM(send_faces.shape, jnp.int32),
             pltpu.SMEM(send_count.shape, jnp.int32),
             pltpu.SemaphoreType.DMA((3,)),
@@ -382,8 +370,6 @@
     from_next = passed_along(back, "space", -1)
 
     sources, levels = source_face.T, subface.T
-    lifts = jnp.asarray(mortar_lifts())
-    gradient = jnp.asarray(gradients.reshape(3 * nodes, nodes), jnp.bfloat16)
     indices = pltpu.SMEM(sources.shape, jnp.int32)
     part, left = pl.pallas_call(
         local_kernel,
@@ -391,19 +377,17 @@
             pltpu.VMEM(dist.shape, jnp.float32),
             pltpu.VMEM((elements, 3 * nodes, 128), jnp.bfloat16),
         ),
-        in_specs=[in_hbm()] * 3 + [in_vmem()] * 2,
+        in_specs=[in_hbm()] * 2 + [in_vmem()] * 3,
         out_specs=(in_vmem(), in_vmem()),
         scratch_shapes=[
-            block,
-            pltpu.VMEM((faces + 1, 16, width), jnp.bfloat16),
             pltpu.VMEM((elements, 128, width), jnp.bfloat16),
             indices,
             indices,
-            pltpu.SemaphoreType.DMA((3,)),
+            pltpu.SemaphoreType.DMA((2,)),
         ],
         compiler_params=pltpu.CompilerParams(vmem_limit_bytes=SCOPED),
         name="transport_local",
-    )(*off_chip(sources, levels, dist), on_chip(gradient), on_chip(lifts))
+    )(*off_chip(sources, levels), on_chip(held), on_chip(rows), on_chip(jnp.asarray(transport_tables())))
     updated = pl.pallas_call(
         remote_kernel,
         out_shape=block,

time: 73.2 us -> 72.7 us (level)
  local copies, waits for them, and re-layouts: 1.62 us -> 0.82 us
    unnamed x13 -> x11, local copies, waits for them, and re-layouts: 1.62 us -> 0.82 us
  transfers between devices with their start and end apart: 2 -> 2, of which waited for: 0 -> 1; matrix products, arithmetic and copies ran while one was open for 0% -> 0% of each run, Pallas kernels for 3% -> 2%
where the time goes in v4:
time: 72.7 us; the launch traced here: 72.3 us
  blocking collectives  45.9 us (63%)
  starting transfers between devices  15.6 us (21%)
  Pallas kernels  9.53 us (13%)
  local copies, waits for them, and re-layouts  0.82 us (1%)
    all_to_all x1, blocking collectives, on_device(): lax.all_to_all(updated, 'vel', split_axis=0, concat_axis=0, tiled=True)  25.9 us
    all_to_all x1, blocking collectives, on_device(): return lax.all_to_all(mixed, 'vel', split_axis=0, concat_axis=0, tiled=True)  20 us
    ppermute x2, starting transfers between devices, passed_along(): return lax.ppermute(block, axis, route)  15.6 us
    pallas_call x1, Pallas kernels, on_device(): pl.pallas_call(collide_kernel, out_shape=pltpu.VMEM(whole.shape, jnp.bflo...  4.91 us
    pallas_call x1, Pallas kernels, on_device(): pl.pallas_call(local_kernel, out_shape=(pltpu.VMEM(dist.shape, jnp.float3...  1.78 us
    pallas_call x1, Pallas kernels, on_device(): pl.pallas_call(send_kernel, out_shape=(traces, traces, block, pltpu.VMEM(...  1.55 us
  transfers between devices with their start and end apart: 2, of which 1 were waited for; matrix products, arithmetic and copies ran while one was open for 0% of the time, Pallas kernels for 2%

profile of v4, /device:TPU:1, one launch (start us, length us, event | category | flops | bytes accessed | tf_op | source)
XLA Modules:
  0.0 72.3 jit_solution(17380399484495397678)
XLA Ops:
  0.0 0.0 copy-start
  0.0 1.6 %send_traces.1 = (bf16[16,16,256]{2,1,0:T(8,128)(2,1)S(1)}, bf16[16,16,256]{2,1,0:T(8,128)(2,1)S(1)}, bf16[16,64,256]{2,1,0:T(8,128)(2,1)S(1)}, bf16[97,16,256]{2,1,0:T(8,128)(2,1)S(1)}) custom-call(s32[1,2,16]{2,1,0:T(2,128)} %faces_hbm.1, s32[1,2]{1,0:T(1,128)} %count_hbm.1, bf16[16,64,256]{2,1,0:T(8,128)(2,1)} %dist_hbm.1), custom_call_target="tpu_custom_call" | custom-call | tf_op jit(solution)/shard_map/send_traces/pallas_call | solution.py:356
  1.6 3.9 %collective-permute-start = (bf16[16,16,256]{2,1,0:T(8,128)(2,1)S(1)}, bf16[16,16,256]{2,1,0:T(8,128)(2,1)S(1)}, u32[]{:S(2)}, u32[]{:S(2)}) collective-permute-start(bf16[16,16,256]{2,1,0:T(8,128)(2,1)S(1)} %get-tuple-element.15), channel_id=1, source_target_pairs={{496,0},{0,16},{16,32},{32,48},{48,64},{64,80},{80,96},{96,112},{1... | collective-permute-start | bytes 393224 | tf_op jit(solution)/shard_map/ppermute | solution.py:24
  5.5 11.7 %collective-permute-start.1 = (bf16[16,16,256]{2,1,0:T(8,128)(2,1)S(1)}, bf16[16,16,256]{2,1,0:T(8,128)(2,1)S(1)}, u32[]{:S(2)}, u32[]{:S(2)}) collective-permute-start(bf16[16,16,256]{2,1,0:T(8,128)(2,1)S(1)} %get-tuple-element.16), channel_id=1, source_target_pairs={{16,0},{32,16},{48,32},{64,48},{80,64},{96,80},{112,96},{128,112},... | collective-permute-start | bytes 393224 | tf_op jit(solution)/shard_map/ppermute | solution.py:24
  17.2 0.0 copy-done
  17.2 1.8 %transport_local.1 = (f32[16,64,256]{2,1,0:T(8,128)S(1)}, bf16[16,192,128]{2,1,0:T(8,128)(2,1)S(1)}) custom-call(s32[6,16]{1,0:T(8,128)} %bitcast.2, s32[6,16]{1,0:T(8,128)} %bitcast.4, bf16[16,64,256]{2,1,0:T(8,128)(2,1)S(1)} %get-tuple-element.11.held, bf16[97,16,256]{2,1,0:T(8,128)(2,1)S(1)} %get-tuple-element.12.rows, bf16[33,64,128]{2,1,0:T(8,128)(2,1)S(1)} %copy-done), custom_call_target="tpu_custom_call" | custom-call | tf_op jit(solution)/shard_map/transport_local/pallas_call | solution.py:374
  19.0 0.0 collective-permute-done.prev_ref
  19.0 0.3 collective-permute-done.1.next_ref
  19.3 1.3 %transport_remote.1 = bf16[16,64,256]{2,1,0:T(8,128)(2,1)S(1)} custom-call(s32[6,16]{1,0:T(8,128)} %bitcast.3, f32[16,64,256]{2,1,0:T(8,128)S(1)} %get-tuple-element.13.part_ref, bf16[16,192,128]{2,1,0:T(8,128)(2,1)S(1)} %get-tuple-element.14.left_ref, bf16[16,16,256]{2,1,0:T(8,128)(2,1)S(1)} %collective-permute-done.prev_ref, ...), custom_call_target="tpu_custom_call" | custom-call | tf_op jit(solution)/shard_map/transport_remote/pallas_call | solution.py:391
  20.6 0.0 copy-start.1
  20.6 0.0 copy-start.2
  20.6 0.0 copy-start.3
  20.7 0.0 copy-start.4
  20.7 25.9 %all_to_all.10.dist_ref = bf16[16,64,256]{2,1,0:T(8,128)(2,1)S(1)} all-to-all(bf16[16,64,256]{2,1,0:T(8,128)(2,1)S(1)} %transport_remote.1), channel_id=1, replica_groups=mesh['space'=32,'vel'=16] {'vel'}, dimensions={0} | all-to-all | bytes 1048576 | tf_op jit(solution)/shard_map/all_to_all | solution.py:411
  46.6 0.0 copy-done.1
  46.6 0.0 copy-done.2
  46.6 0.0 copy-done.3
  46.6 0.0 copy-done.4
  46.6 4.9 %collide.1 = bf16[16,64,256]{2,1,0:T(8,128)(2,1)S(1)} custom-call(bf16[16,64,256]{2,1,0:T(8,128)(2,1)S(1)} %all_to_all.10.dist_ref, f32[4,4096]{1,0:T(4,128)S(1)} %copy-done.4, f32[5,4096]{1,0:T(8,128)S(1)} %copy-done.3, bf16[2,256,256]{2,1,0:T(8,128)(2,1)S(1)} %copy-done.2, bf16[2,256,256]{2,1,0:T(8,128)(2,1)S(1)} %copy-done.1), custom_call_target="tpu_custom_call" | custom-call | tf_op jit(solution)/shard_map/collide/pallas_call | solution.py:413
  51.5 20.0 %all_to_all.11 = bf16[16,64,256]{2,1,0:T(8,128)(2,1)S(1)} all-to-all(bf16[16,64,256]{2,1,0:T(8,128)(2,1)S(1)} %collide.1), channel_id=1, replica_groups=mesh['space'=32,'vel'=16] {'vel'}, dimensions={0} | all-to-all | bytes 1048576 | tf_op jit(solution)/shard_map/all_to_all | solution.py:422
  71.5 0.8 %copy.12 = bf16[16,64,256]{2,1,0:T(8,128)(2,1)} copy(bf16[16,64,256]{2,1,0:T(8,128)(2,1)S(1)} %all_to_all.11) | data formatting | bytes 1048576
Async XLA Ops:
  0.0 17.2 %copy-start = (bf16[33,64,128]{2,1,0:T(8,128)(2,1)S(1)}, bf16[33,64,128]{2,1,0:T(8,128)(2,1)}, u32[]{:S(2)}) copy-start(bf16[33,64,128]{2,1,0:T(8,128)(2,1)} %constant.6.clone.table_ref) | copy-start | bytes 1622020
  1.6 17.4 %collective-permute-start = (bf16[16,16,256]{2,1,0:T(8,128)(2,1)S(1)}, bf16[16,16,256]{2,1,0:T(8,128)(2,1)S(1)}, u32[]{:S(2)}, u32[]{:S(2)}) collective-permute-start(bf16[16,16,256]{2,1,0:T(8,128)(2,1)S(1)} %get-tuple-element.15), channel_id=1, source_target_pairs={{496,0},{0,16},{16,32},{32,48},{48,64},{64,80},{80,96},{96,112},{1... | collective-permute-start | bytes 393224 | tf_op jit(solution)/shard_map/ppermute | solution.py:24
  5.5 13.8 %collective-permute-start.1 = (bf16[16,16,256]{2,1,0:T(8,128)(2,1)S(1)}, bf16[16,16,256]{2,1,0:T(8,128)(2,1)S(1)}, u32[]{:S(2)}, u32[]{:S(2)}) collective-permute-start(bf16[16,16,256]{2,1,0:T(8,128)(2,1)S(1)} %get-tuple-element.16), channel_id=1, source_target_pairs={{16,0},{32,16},{48,32},{64,48},{80,64},{96,80},{112,96},{128,112},... | collective-permute-start | bytes 393224 | tf_op jit(solution)/shard_map/ppermute | solution.py:24
  20.6 26.0 %copy-start.1 = (bf16[2,256,256]{2,1,0:T(8,128)(2,1)S(1)}, bf16[2,256,256]{2,1,0:T(8,128)(2,1)}, u32[]{:S(2)}) copy-start(bf16[2,256,256]{2,1,0:T(8,128)(2,1)} %constant.8.clone.back_ref) | copy-start | bytes 786436
  20.6 26.0 %copy-start.2 = (bf16[2,256,256]{2,1,0:T(8,128)(2,1)S(1)}, bf16[2,256,256]{2,1,0:T(8,128)(2,1)}, u32[]{:S(2)}) copy-start(bf16[2,256,256]{2,1,0:T(8,128)(2,1)} %constant.7.clone.into_ref) | copy-start | bytes 786436
  20.6 26.0 %copy-start.3 = (f32[5,4096]{1,0:T(8,128)S(1)}, f32[5,4096]{1,0:T(8,128)}, u32[]{:S(2)}) copy-start(f32[5,4096]{1,0:T(8,128)} %beta_ref.1) | copy-start | bytes 245764
  20.7 25.9 %copy-start.4 = (f32[4,4096]{1,0:T(4,128)S(1)}, f32[4,4096]{1,0:T(4,128)}, u32[]{:S(2)}) copy-start(f32[4,4096]{1,0:T(4,128)} %alpha_ref.1) | copy-start | bytes 196612

commit v5 on v4

--- a/solution.py
+++ b/solution.py
@@ -200,8 +200,24 @@
         rows[6 * at : 6 * at + 6] = traces.reshape(6, 16, width)
 
 
-def send_kernel(faces_hbm, count_hbm, dist_hbm, back_ref, ahead_ref, held, rows, faces, count, sems):
-    copies = fetched(sems, (faces_hbm, faces), (count_hbm, count), (dist_hbm, held))
+def send_kernel(
+    faces_hbm,
+    count_hbm,
+    source_hbm,
+    level_hbm,
+    dist_hbm,
+    back_ref,
+    ahead_ref,
+    held,
+    rows,
+    source,
+    level,
+    faces,
+    count,
+    sems,
+):
+    pairs = (faces_hbm, faces), (count_hbm, count), (dist_hbm, held), (source_hbm, source)
+    copies = fetched(sems, *pairs, (level_hbm, level))
     for copy in copies:
         copy.wait()
     extract_traces(held, rows)
@@ -221,10 +237,7 @@
     return total
 
 
-def local_kernel(
-    source_hbm, level_hbm, held, rows, table_ref, out_ref, left_ref, stack, source, level, sems
-):
-    copies = fetched(sems, (source_hbm, source), (level_hbm, level))
+def local_kernel(source, level, held, rows, table_ref, out_ref, left_ref, stack):
     elements, nodes, width = held.shape
     faces = 6 * elements
     speeds = local_speeds((1, width))
@@ -237,8 +250,6 @@
         member = jnp.logical_and(on, digits[face // 2] == 3 * (face % 2))
         loss = loss + jnp.where(member, jnp.abs(wide[face // 2]), 0.0)
     keep = 1.0 - courant * lift_weight * loss
-    for copy in copies:
-        copy.wait()
     gradient = table_ref[30:].reshape(3 * nodes, table_ref.shape[2])[:, :nodes]
     for at in range(elements):
         for face in range(6):
@@ -261,18 +272,13 @@
         out_ref[at] = add_lifts(left, stack[at], total)
 
 
-def remote_kernel(
-    source_hbm, part_ref, left_ref, prev_ref, next_ref, out_ref, table, stack, source, sems
-):
-    copies = fetched(sems, (source_hbm, source))
+def remote_kernel(source, part_ref, left_ref, prev_ref, next_ref, out_ref, table, stack):
     elements, _, width = part_ref.shape
     faces = 6 * elements
     table[0] = jnp.zeros((16, width), jnp.bfloat16)
     table[1 : SLOTS + 1] = prev_ref[...]
     table[SLOTS + 1 :] = next_ref[...]
     masks = inflow_masks((16, width))
-    for copy in copies:
-        copy.wait()
     for at in range(elements):
         for face in range(6):
             trace = table[jnp.maximum(source[face, at] - (faces - 1), 0)] * masks[face]
@@ -281,54 +287,38 @@
         out_ref[at] = add_lifts(left_ref[at], stack[at], part_ref[at]).astype(jnp.bfloat16)
 
 
-def collide_kernel(
-    dist_ref, alpha_ref, beta_ref, into_ref, back_ref, out_ref, spectrum, fields, first, gain
-):
+def collide_kernel(dist_ref, alpha_ref, beta_ref, into_ref, back_ref, out_ref):
     nodes, plane = dist_ref.shape[1], dist_ref.shape[2]
     modes = alpha_ref.shape[0]
-    order = [m for pair in range(modes) for m in (pair, modes + pair)] + [2 * modes]
-    halves = [slice(0, plane // 2), slice(plane // 2, plane)]
-
-    def planes(slot, lanes):
-        return [fields[slot, i * GROUP : (i + 1) * GROUP, lanes] for i in range(VSIDE)]
+
+    def planes(array):
+        cube = array.reshape(VSIDE, GROUP, plane)
+        return [cube[i] for i in range(VSIDE)]
 
     for start in range(0, nodes, GROUP):
         group = slice(start, start + GROUP)
         values = dist_ref[:, group, :].reshape(VSIDE * GROUP, plane)
-        fields[0] = dot(values, into_ref[0]) + dot(values, into_ref[1])
-        for lanes in halves:
-            for i, part in enumerate(cosine_forward(planes(0, lanes))):
-                spectrum[i, :, lanes] = part if i else 0.5 * part
-
-        def filtered(which, slot):
-            kern = alpha_ref if which < modes else beta_ref
-            row = which % modes if which < 2 * modes else modes
+        spectrum = cosine_forward(planes(dot(values, into_ref[0]) + dot(values, into_ref[1])))
+        spectrum[0] = 0.5 * spectrum[0]
+
+        def field(kern, row):
             parts = [
                 (spectrum[i] * kern[row : row + 1, i * plane : (i + 1) * plane]).astype(jnp.bfloat16)
                 for i in range(VSIDE)
             ]
             left = jnp.concatenate(parts, axis=0)
-            fields[slot] = dot(left, back_ref[0]) + dot(left, back_ref[1])
-
-        def gathered(which, slot):
-            for lanes in halves:
-                for i, field in enumerate(cosine_backward(planes(slot, lanes))):
-                    if which < modes:
-                        first[i, :, lanes] = field
-                    elif which == modes:
-                        gain[i, :, lanes] = first[i, :, lanes] * field
-                    elif which < 2 * modes:
-                        gain[i, :, lanes] = gain[i, :, lanes] + first[i, :, lanes] * field
-                    else:
-                        value = dist_ref[i, group, lanes].astype(jnp.float32)
-                        total = value + relax_step * (gain[i, :, lanes] - value * field)
-                        out_ref[i, group, lanes] = total.astype(jnp.bfloat16)
-
-        filtered(order[0], 0)
-        for at, which in enumerate(order):
-            if at + 1 < len(order):
-                filtered(order[at + 1], (at + 1) % 2)
-            gathered(which, at % 2)
+            return cosine_backward(planes(dot(left, back_ref[0]) + dot(left, back_ref[1])))
+
+        gain = None
+        for mode in range(modes):
+            pairs = zip(field(alpha_ref, mode), field(beta_ref, mode))
+            products = [first * second for first, second in pairs]
+            gain = products if mode == 0 else [a + b for a, b in zip(gain, products)]
+        loss = field(beta_ref, modes)
+        for i in range(VSIDE):
+            value = dist_ref[i, group, :].astype(jnp.float32)
+            total = value + relax_step * (gain[i] - value * loss[i])
+            out_ref[i, group, :] = total.astype(jnp.bfloat16)
 
 
 def in_vmem():
@@ -339,8 +329,16 @@
     return pl.BlockSpec(memory_space=pltpu.HBM)
 
 
-def on_chip(array):
-    return pltpu.with_memory_space_constraint(array, pltpu.VMEM)
+def in_smem():
+    return pl.BlockSpec(memory_space=pltpu.SMEM)
+
+
+def on_chip(*arrays):
+    return [pltpu.with_memory_space_constraint(array, pltpu.VMEM) for array in arrays]
+
+
+def in_scalar(*arrays):
+    return [pltpu.with_memory_space_constraint(array, pltpu.SMEM) for array in arrays]
 
 
 def off_chip(*arrays):
@@ -353,55 +351,56 @@
     traces = pltpu.VMEM((SLOTS, 16, width), jnp.bfloat16)
     block = pltpu.VMEM(dist.shape, jnp.bfloat16)
 
-    back, ahead, held, rows = pl.pallas_call(
+    sources, levels = source_face.T, subface.T
+    indices = pltpu.SMEM(sources.shape, jnp.int32)
+    back, ahead, held, rows, source, level = pl.pallas_call(
         send_kernel,
-        out_shape=(traces, traces, block, pltpu.VMEM((faces + 1, 16, width), jnp.bfloat16)),
-        in_specs=[in_hbm()] * 3,
-        out_specs=(in_vmem(),) * 4,
+        out_shape=(
+            traces,
+            traces,
+            block,
+            pltpu.VMEM((faces + 1, 16, width), jnp.bfloat16),
+            indices,
+            indices,
+        ),
+        in_specs=[in_hbm()] * 5,
+        out_specs=(in_vmem(),) * 4 + (in_smem(),) * 2,
         scratch_shapes=[
             pltpu.SMEM(send_faces.shape, jnp.int32),
             pltpu.SMEM(send_count.shape, jnp.int32),
-            pltpu.SemaphoreType.DMA((3,)),
+            pltpu.SemaphoreType.DMA((5,)),
         ],
         compiler_params=pltpu.CompilerParams(vmem_limit_bytes=SCOPED),
         name="send_traces",
-    )(*off_chip(send_faces, send_count, dist))
+    )(*off_chip(send_faces, send_count, sources, levels, dist))
     from_prev = passed_along(ahead, "space", 1)
     from_next = passed_along(back, "space", -1)
 
-    sources, levels = source_face.T, subface.T
-    indices = pltpu.SMEM(sources.shape, jnp.int32)
+    source, level = in_scalar(source, level)
     part, left = pl.pallas_call(
         local_kernel,
         out_shape=(
             pltpu.VMEM(dist.shape, jnp.float32),
             pltpu.VMEM((elements, 3 * nodes, 128), jnp.bfloat16),
         ),
-        in_specs=[in_hbm()] * 2 + [in_vmem()] * 3,
+        in_specs=[in_smem()] * 2 + [in_vmem()] * 3,
         out_specs=(in_vmem(), in_vmem()),
-        scratch_shapes=[
-            pltpu.VMEM((elements, 128, width), jnp.bfloat16),
-            indices,
-            indices,
-            pltpu.SemaphoreType.DMA((2,)),
-        ],
+        scratch_shapes=[pltpu.VMEM((elements, 128, width), jnp.bfloat16)],
         compiler_params=pltpu.CompilerParams(vmem_limit_bytes=SCOPED),
         name="transport_local",
-    )(*off_chip(sources, levels), on_chip(held), on_chip(rows), on_chip(jnp.asarray(transport_tables())))
+    )(source, level, *on_chip(held, rows, jnp.asarray(transport_tables())))
     updated = pl.pallas_call(
         remote_kernel,
         out_shape=block,
-        in_specs=[in_hbm()] + [in_vmem()] * 4,
+        in_specs=[in_smem()] + [in_vmem()] * 4,
         out_specs=in_vmem(),
         scratch_shapes=[
             pltpu.VMEM((2 * SLOTS + 1, 16, width), jnp.bfloat16),
             pltpu.VMEM((elements, 128, width), jnp.bfloat16),
-            indices,
-            pltpu.SemaphoreType.DMA((1,)),
         ],
         compiler_params=pltpu.CompilerParams(vmem_limit_bytes=SCOPED),
         name="transport_remote",
-    )(*off_chip(sources), on_chip(part), on_chip(left), on_chip(from_prev), on_chip(from_next))
+    )(source, *on_chip(part, left, from_prev, from_next))
 
     plane = VSIDE * VSIDE
     cosine = cosine_table()
@@ -409,16 +408,14 @@
     into = jnp.asarray(np.stack(split_table(pair.T * (2.0 / VSIDE))))
     out_of = jnp.asarray(np.stack(split_table(pair)))
     whole = lax.all_to_all(updated, "vel", split_axis=0, concat_axis=0, tiled=True)
-    cube = pltpu.VMEM((VSIDE, GROUP, plane), jnp.float32)
     mixed = pl.pallas_call(
         collide_kernel,
         out_shape=pltpu.VMEM(whole.shape, jnp.bfloat16),
         in_specs=[in_vmem()] * 5,
         out_specs=in_vmem(),
-        scratch_shapes=[cube, pltpu.VMEM((2, VSIDE * GROUP, plane), jnp.float32), cube, cube],
         compiler_params=pltpu.CompilerParams(vmem_limit_bytes=SCOPED),
         name="collide",
-    )(*[on_chip(array) for array in (whole, alpha, beta, into, out_of)])
+    )(*on_chip(whole, alpha, beta, into, out_of))
     return lax.all_to_all(mixed, "vel", split_axis=0, concat_axis=0, tiled=True)
 
 

time: 72.7 us -> 71.7 us (0.986)
  Pallas kernels: 9.53 us -> 7.89 us
  transfers between devices with their start and end apart: 2 -> 2, of which waited for: 1 -> 2; matrix products, arithmetic and copies ran while one was open for 0% -> 0% of each run, Pallas kernels for 2% -> 1%
where the time goes in v5:
time: 71.7 us; the launch traced here: 71.4 us
  blocking collectives  45.9 us (64%)
  starting transfers between devices  15.6 us (22%)
  Pallas kernels  7.89 us (11%)
  waiting for transfers between devices  1.05 us (1%)
  local copies, waits for them, and re-layouts  0.82 us (1%)
    all_to_all x1, blocking collectives, on_device(): lax.all_to_all(updated, 'vel', split_axis=0, concat_axis=0, tiled=True)  25.9 us
    all_to_all x1, blocking collectives, on_device(): return lax.all_to_all(mixed, 'vel', split_axis=0, concat_axis=0, tiled=True)  20 us
    ppermute x2, starting transfers between devices, passed_along(): return lax.ppermute(block, axis, route)  15.6 us
    pallas_call x1, Pallas kernels, on_device(): pl.pallas_call(collide_kernel, out_shape=pltpu.VMEM(whole.shape, jnp.bflo...  4.65 us
    pallas_call x1, Pallas kernels, on_device(): pl.pallas_call(send_kernel, out_shape=(traces, traces, block, pltpu.VMEM(...  1.58 us
  transfers between devices with their start and end apart: 2, of which 2 were waited for; matrix products, arithmetic and copies ran while one was open for 0% of the time, Pallas kernels for 1%

profile of v5, /device:TPU:1, one launch (start us, length us, event | category | flops | bytes accessed | tf_op | source)
XLA Modules:
  0.0 71.4 jit_solution(13011866672306800534)
XLA Ops:
  0.0 0.0 copy-start
  0.0 1.6 %send_traces.1 = (bf16[16,16,256]{2,1,0:T(8,128)(2,1)S(1)}, bf16[16,16,256]{2,1,0:T(8,128)(2,1)S(1)}, bf16[16,64,256]{2,1,0:T(8,128)(2,1)S(1)}, bf16[97,16,256]{...) custom-call(s32[1,2,16]{2,1,0:T(2,128)} %faces_hbm.1, s32[1,2]{1,0:T(1,128)} %count_hbm.1, ...), custom_call_target="tpu_custom_call" | custom-call | tf_op jit(solution)/shard_map/send_traces/pallas_call | solution.py:356
  1.6 4.0 %collective-permute-start = (bf16[16,16,256]{2,1,0:T(8,128)(2,1)S(1)}, bf16[16,16,256]{2,1,0:T(8,128)(2,1)S(1)}, u32[]{:S(2)}, u32[]{:S(2)}) collective-permute-start(bf16[16,16,256]{2,1,0:T(8,128)(2,1)S(1)} %get-tuple-element.19), channel_id=1, source_target_pairs={{496,0},{0,16},{16,32},{32,48},{48,64},{64,80},{80,96},{96,112},{1... | collective-permute-start | bytes 393224 | tf_op jit(solution)/shard_map/ppermute | solution.py:24
  5.5 11.7 %collective-permute-start.1 = (bf16[16,16,256]{2,1,0:T(8,128)(2,1)S(1)}, bf16[16,16,256]{2,1,0:T(8,128)(2,1)S(1)}, u32[]{:S(2)}, u32[]{:S(2)}) collective-permute-start(bf16[16,16,256]{2,1,0:T(8,128)(2,1)S(1)} %get-tuple-element.20), channel_id=1, source_target_pairs={{16,0},{32,16},{48,32},{64,48},{80,64},{96,80},{112,96},{128,112},... | collective-permute-start | bytes 393224 | tf_op jit(solution)/shard_map/ppermute | solution.py:24
  17.2 0.0 copy-done
  17.2 1.1 %transport_local.1 = (f32[16,64,256]{2,1,0:T(8,128)S(1)}, bf16[16,192,128]{2,1,0:T(8,128)(2,1)S(1)}) custom-call(s32[6,16]{1,0:T(8,128)S(4)} %get-tuple-element.13.source, s32[6,16]{1,0:T(8,128)S(4)} %get-tuple-element.14.level, bf16[16,64,256]{2,1,0:T(8,128)(2,1)S(1)} %get-tuple-element.15.held, bf16[97,16,256]{2,1,0:T(8,128)(2,1)S(1)} %get-tuple-element.16.rows, ...), custom_call_target="tpu_custom_call" | custom-call | tf_op jit(solution)/shard_map/transport_local/pallas_call | solution.py:380
  18.3 0.2 collective-permute-done.prev_ref
  18.5 0.9 %collective-permute-done.1.next_ref = bf16[16,16,256]{2,1,0:T(8,128)(2,1)S(1)} collective-permute-done((bf16[16,16,256]{2,1,0:T(8,128)(2,1)S(1)}, bf16[16,16,256]{2,1,0:T(8,128)(2,1)S(1)}, u32[]{:S(2)}, u32[]{:S(2)}) %collective-permute-start.1) | collective-permute-done | bytes 131104 | tf_op jit(solution)/shard_map/ppermute | solution.py:24
  19.4 0.6 transport_remote.1
  20.0 0.0 copy-start.1
  20.0 0.0 copy-start.2
  20.0 0.0 copy-start.3
  20.0 0.0 copy-start.4
  20.0 25.9 %all_to_all.10.dist_ref = bf16[16,64,256]{2,1,0:T(8,128)(2,1)S(1)} all-to-all(bf16[16,64,256]{2,1,0:T(8,128)(2,1)S(1)} %transport_remote.1), channel_id=1, replica_groups=mesh['space'=32,'vel'=16] {'vel'}, dimensions={0} | all-to-all | bytes 1048576 | tf_op jit(solution)/shard_map/all_to_all | solution.py:410
  45.9 0.0 copy-done.1
  45.9 0.0 copy-done.2
  45.9 0.0 copy-done.3
  45.9 0.0 copy-done.4
  45.9 4.6 %collide.1 = bf16[16,64,256]{2,1,0:T(8,128)(2,1)S(1)} custom-call(bf16[16,64,256]{2,1,0:T(8,128)(2,1)S(1)} %all_to_all.10.dist_ref, f32[4,4096]{1,0:T(4,128)S(1)} %copy-done.4, f32[5,4096]{1,0:T(8,128)S(1)} %copy-done.3, bf16[2,256,256]{2,1,0:T(8,128)(2,1)S(1)} %copy-done.2, bf16[2,256,256]{2,1,0:T(8,128)(2,1)S(1)} %copy-done.1), custom_call_target="tpu_custom_call" | custom-call | tf_op jit(solution)/shard_map/collide/pallas_call | solution.py:411
  50.6 20.0 %all_to_all.11 = bf16[16,64,256]{2,1,0:T(8,128)(2,1)S(1)} all-to-all(bf16[16,64,256]{2,1,0:T(8,128)(2,1)S(1)} %collide.1), channel_id=1, replica_groups=mesh['space'=32,'vel'=16] {'vel'}, dimensions={0} | all-to-all | bytes 1048576 | tf_op jit(solution)/shard_map/all_to_all | solution.py:419
  70.6 0.8 %copy.12 = bf16[16,64,256]{2,1,0:T(8,128)(2,1)} copy(bf16[16,64,256]{2,1,0:T(8,128)(2,1)S(1)} %all_to_all.11) | data formatting | bytes 1048576
Async XLA Ops:
  0.0 17.2 %copy-start = (bf16[33,64,128]{2,1,0:T(8,128)(2,1)S(1)}, bf16[33,64,128]{2,1,0:T(8,128)(2,1)}, u32[]{:S(2)}) copy-start(bf16[33,64,128]{2,1,0:T(8,128)(2,1)} %constant.6.clone.table_ref) | copy-start | bytes 1622020
  1.6 16.9 %collective-permute-start = (bf16[16,16,256]{2,1,0:T(8,128)(2,1)S(1)}, bf16[16,16,256]{2,1,0:T(8,128)(2,1)S(1)}, u32[]{:S(2)}, u32[]{:S(2)}) collective-permute-start(bf16[16,16,256]{2,1,0:T(8,128)(2,1)S(1)} %get-tuple-element.19), channel_id=1, source_target_pairs={{496,0},{0,16},{16,32},{32,48},{48,64},{64,80},{80,96},{96,112},{1... | collective-permute-start | bytes 393224 | tf_op jit(solution)/shard_map/ppermute | solution.py:24
  5.5 13.8 %collective-permute-start.1 = (bf16[16,16,256]{2,1,0:T(8,128)(2,1)S(1)}, bf16[16,16,256]{2,1,0:T(8,128)(2,1)S(1)}, u32[]{:S(2)}, u32[]{:S(2)}) collective-permute-start(bf16[16,16,256]{2,1,0:T(8,128)(2,1)S(1)} %get-tuple-element.20), channel_id=1, source_target_pairs={{16,0},{32,16},{48,32},{64,48},{80,64},{96,80},{112,96},{128,112},... | collective-permute-start | bytes 393224 | tf_op jit(solution)/shard_map/ppermute | solution.py:24
  20.0 26.0 %copy-start.1 = (bf16[2,256,256]{2,1,0:T(8,128)(2,1)S(1)}, bf16[2,256,256]{2,1,0:T(8,128)(2,1)}, u32[]{:S(2)}) copy-start(bf16[2,256,256]{2,1,0:T(8,128)(2,1)} %constant.8.clone.back_ref) | copy-start | bytes 786436
  20.0 26.0 %copy-start.2 = (bf16[2,256,256]{2,1,0:T(8,128)(2,1)S(1)}, bf16[2,256,256]{2,1,0:T(8,128)(2,1)}, u32[]{:S(2)}) copy-start(bf16[2,256,256]{2,1,0:T(8,128)(2,1)} %constant.7.clone.into_ref) | copy-start | bytes 786436
  20.0 26.0 %copy-start.3 = (f32[5,4096]{1,0:T(8,128)S(1)}, f32[5,4096]{1,0:T(8,128)}, u32[]{:S(2)}) copy-start(f32[5,4096]{1,0:T(8,128)} %beta_ref.1) | copy-start | bytes 245764
  20.0 25.9 %copy-start.4 = (f32[4,4096]{1,0:T(4,128)S(1)}, f32[4,4096]{1,0:T(4,128)}, u32[]{:S(2)}) copy-start(f32[4,4096]{1,0:T(4,128)} %alpha_ref.1) | copy-start | bytes 196612

commit v6 on v5

--- a/solution.py
+++ b/solution.py
@@ -16,12 +16,6 @@
 courant = 0.1
 lift_weight = 6.0
 relax_step = 0.5
-
-
-def passed_along(block, axis, distance):
-    devices = range(lax.axis_size(axis))
-    route = [((i - distance) % len(devices), i) for i in devices]
-    return lax.ppermute(block, axis, route)
 
 
 def lobatto_points():
@@ -206,8 +200,8 @@
     source_hbm,
     level_hbm,
     dist_hbm,
-    back_ref,
-    ahead_ref,
+    near_ref,
+    far_ref,
     held,
     rows,
     source,
@@ -221,25 +215,22 @@
     for copy in copies:
         copy.wait()
     extract_traces(held, rows)
-    rows[6 * held.shape[0]] = jnp.zeros(rows.shape[1:], jnp.bfloat16)
-    for way, out in enumerate((back_ref, ahead_ref)):
+    near_way = 1 - (lax.axis_index("space") & 1)
+    for way, out in ((1 - near_way, far_ref), (near_way, near_ref)):
         for slot in range(SLOTS):
             keep = jnp.where(slot < count[0, way], 1.0, 0.0).astype(jnp.bfloat16)
             out[slot] = rows[faces[0, way, slot]] * keep
 
 
-def add_lifts(left, stacked, total):
-    speeds = local_speeds((1, total.shape[-1]))
-    lifted = dot(left, stacked)
-    for axis in range(3):
-        weight = -courant * lift_weight * speeds[axis]
-        total = total + lifted[64 * axis : 64 * axis + 64] * weight
-    return total
-
-
-def local_kernel(source, level, held, rows, table_ref, out_ref, left_ref, stack):
+def transport_kernel(
+    source, level, held, rows, near_ref, far_ref, table_ref, out_ref, traces, stack
+):
     elements, nodes, width = held.shape
     faces = 6 * elements
+    odd = lax.axis_index("space") & 1
+    traces[:faces] = rows[...]
+    traces[pl.ds(faces + SLOTS * (1 - odd), SLOTS)] = near_ref[pl.ds(SLOTS * (1 - odd), SLOTS)]
+    traces[pl.ds(faces + SLOTS * odd, SLOTS)] = far_ref[...]
     speeds = local_speeds((1, width))
     masks = inflow_masks((16, width))
     wide = local_speeds((nodes, width))
@@ -253,13 +244,9 @@
     gradient = table_ref[30:].reshape(3 * nodes, table_ref.shape[2])[:, :nodes]
     for at in range(elements):
         for face in range(6):
-            trace = rows[jnp.minimum(source[face, at], faces)] * masks[face]
+            trace = traces[source[face, at]] * masks[face]
             stack[at, 16 * face : 16 * face + 16] = trace
         stack[at, 96:] = jnp.zeros((32, width), jnp.bfloat16)
-        total = held[at].astype(jnp.float32) * keep
-        moved = dot(gradient, held[at])
-        for axis in range(3):
-            total = total + moved[64 * axis : 64 * axis + 64] * (-courant * speeds[axis])
         left = jnp.concatenate(
             [
                 table_ref[10 * axis + level[2 * axis, at]]
@@ -268,23 +255,14 @@
             ],
             axis=0,
         )
-        left_ref[at] = left
-        out_ref[at] = add_lifts(left, stack[at], total)
-
-
-def remote_kernel(source, part_ref, left_ref, prev_ref, next_ref, out_ref, table, stack):
-    elements, _, width = part_ref.shape
-    faces = 6 * elements
-    table[0] = jnp.zeros((16, width), jnp.bfloat16)
-    table[1 : SLOTS + 1] = prev_ref[...]
-    table[SLOTS + 1 :] = next_ref[...]
-    masks = inflow_masks((16, width))
-    for at in range(elements):
-        for face in range(6):
-            trace = table[jnp.maximum(source[face, at] - (faces - 1), 0)] * masks[face]
-            stack[at, 16 * face : 16 * face + 16] = trace
-        stack[at, 96:] = jnp.zeros((32, width), jnp.bfloat16)
-        out_ref[at] = add_lifts(left_ref[at], stack[at], part_ref[at]).astype(jnp.bfloat16)
+        moved = dot(gradient, held[at])
+        lifted = dot(left, stack[at])
+        total = held[at].astype(jnp.float32) * keep
+        for axis in range(3):
+            part = slice(64 * axis, 64 * axis + 64)
+            total = total + moved[part] * (-courant * speeds[axis])
+            total = total + lifted[part] * (-courant * lift_weight * speeds[axis])
+        out_ref[at] = total.astype(jnp.bfloat16)
 
 
 def collide_kernel(dist_ref, alpha_ref, beta_ref, into_ref, back_ref, out_ref):
@@ -353,13 +331,13 @@
 
     sources, levels = source_face.T, subface.T
     indices = pltpu.SMEM(sources.shape, jnp.int32)
-    back, ahead, held, rows, source, level = pl.pallas_call(
+    near, far, held, rows, source, level = pl.pallas_call(
         send_kernel,
         out_shape=(
             traces,
             traces,
             block,
-            pltpu.VMEM((faces + 1, 16, width), jnp.bfloat16),
+            pltpu.VMEM((faces, 16, width), jnp.bfloat16),
             indices,
             indices,
         ),
@@ -373,34 +351,27 @@
         compiler_params=pltpu.CompilerParams(vmem_limit_bytes=SCOPED),
         name="send_traces",
     )(*off_chip(send_faces, send_count, sources, levels, dist))
-    from_prev = passed_along(ahead, "space", 1)
-    from_next = passed_along(back, "space", -1)
-
-    source, level = in_scalar(source, level)
-    part, left = pl.pallas_call(
-        local_kernel,
-        out_shape=(
-            pltpu.VMEM(dist.shape, jnp.float32),
-            pltpu.VMEM((elements, 3 * nodes, 128), jnp.bfloat16),
-        ),
-        in_specs=[in_smem()] * 2 + [in_vmem()] * 3,
-        out_specs=(in_vmem(), in_vmem()),
-        scratch_shapes=[pltpu.VMEM((elements, 128, width), jnp.bfloat16)],
-        compiler_params=pltpu.CompilerParams(vmem_limit_bytes=SCOPED),
-        name="transport_local",
-    )(source, level, *on_chip(held, rows, jnp.asarray(transport_tables())))
+    blocks = lax.axis_size("space")
+    across = [((i + 1) % blocks, ((i ^ 1) + 1) % blocks) for i in range(blocks)]
+    far = lax.ppermute(far, "space", across)
+    couples = [[i, i + 1] for i in range(0, blocks, 2)]
+    near = lax.all_gather(near, "space", axis=0, tiled=True, axis_index_groups=couples)
+
     updated = pl.pallas_call(
-        remote_kernel,
+        transport_kernel,
         out_shape=block,
-        in_specs=[in_smem()] + [in_vmem()] * 4,
+        in_specs=[in_smem()] * 2 + [in_vmem()] * 5,
         out_specs=in_vmem(),
         scratch_shapes=[
-            pltpu.VMEM((2 * SLOTS + 1, 16, width), jnp.bfloat16),
+            pltpu.VMEM((faces + 2 * SLOTS, 16, width), jnp.bfloat16),
             pltpu.VMEM((elements, 128, width), jnp.bfloat16),
         ],
         compiler_params=pltpu.CompilerParams(vmem_limit_bytes=SCOPED),
-        name="transport_remote",
-    )(source, *on_chip(part, left, from_prev, from_next))
+        name="transport",
+    )(
+        *in_scalar(source, level),
+        *on_chip(held, rows, near, far, jnp.asarray(transport_tables())),
+    )
 
     plane = VSIDE * VSIDE
     cosine = cosine_table()

time: 71.7 us -> 73.1 us (1.020)
  blocking collectives: 45.9 us -> 51 us
  starting transfers between devices: 15.6 us -> 13.7 us
  waiting for transfers between devices: 1.05 us -> 0.01 us
    all_gather x0 -> x1, blocking collectives: none -> 4.5 us  [on_device(): lax.all_gather(near, 'space', axis=0, tiled=True, axis_index_groups=couples)]
    ppermute x2 -> x1, starting transfers between devices: 15.6 us -> 13.7 us  [on_device(): far = lax.ppermute(far, 'space', across)]
    ppermute x2 -> x1, waiting for transfers between devices: 1.05 us -> 0.01 us  [on_device(): far = lax.ppermute(far, 'space', across)]
    pallas_call x2 -> x1, Pallas kernels: 1.66 us -> 1.05 us  [on_device(): pl.pallas_call(transport_kernel, out_shape=block, in_specs=[in_smem()] *...]
  transfers between devices with their start and end apart: 2 -> 1, of which waited for: 2 -> 0; matrix products, arithmetic and copies ran while one was open for 0% -> 0% of each run, Pallas kernels for 1% -> 0%
where the time goes in v6:
time: 73.1 us; the launch traced here: 72.8 us
  blocking collectives  51 us (70%)
  starting transfers between devices  13.7 us (19%)
  Pallas kernels  7.28 us (10%)
  local copies, waits for them, and re-layouts  0.82 us (1%)
    all_to_all x1, blocking collectives, on_device(): lax.all_to_all(updated, 'vel', split_axis=0, concat_axis=0, tiled=True)  26.5 us
    all_to_all x1, blocking collectives, on_device(): return lax.all_to_all(mixed, 'vel', split_axis=0, concat_axis=0, tiled=True)  20 us
    ppermute x1, starting transfers between devices, on_device(): far = lax.ppermute(far, 'space', across)  13.7 us
    pallas_call x1, Pallas kernels, on_device(): pl.pallas_call(collide_kernel, out_shape=pltpu.VMEM(whole.shape, jnp.bflo...  4.65 us
    all_gather x1, blocking collectives, on_device(): lax.all_gather(near, 'space', axis=0, tiled=True, axis_index_groups=couples)  4.5 us
    pallas_call x1, Pallas kernels, on_device(): pl.pallas_call(send_kernel, out_shape=(traces, traces, block, pltpu.VMEM(...  1.58 us
  transfers between devices with their start and end apart: 1, of which 0 were waited for; matrix products, arithmetic and copies ran while one was open for 0% of the time, Pallas kernels for 0%

profile of v6, /device:TPU:1, one launch (start us, length us, event | category | flops | bytes accessed | tf_op | source)
XLA Modules:
  0.0 72.8 jit_solution(5699930284681755469)
XLA Ops:
  0.0 0.0 copy-start
  0.0 1.6 %send_traces.1 = (bf16[16,16,256]{2,1,0:T(8,128)(2,1)S(1)}, bf16[16,16,256]{2,1,0:T(8,128)(2,1)S(1)}, bf16[16,64,256]{2,1,0:T(8,128)(2,1)S(1)}, bf16[96,16,256]{...) custom-call(s32[1,2,16]{2,1,0:T(2,128)} %faces_hbm.1, s32[1,2]{1,0:T(1,128)} %count_hbm.1, ...), custom_call_target="tpu_custom_call" | custom-call | tf_op jit(solution)/shard_map/send_traces/pallas_call | solution.py:334
  1.6 13.7 %collective-permute-start = (bf16[16,16,256]{2,1,0:T(8,128)(2,1)S(1)}, bf16[16,16,256]{2,1,0:T(8,128)(2,1)S(1)}, u32[]{:S(2)}, u32[]{:S(2)}) collective-permute-start(bf16[16,16,256]{2,1,0:T(8,128)(2,1)S(1)} %get-tuple-element.16), channel_id=1, source_target_pairs={{16,32},{32,16},{48,64},{64,48},{80,96},{96,80},{112,128},{128,112... | collective-permute-start | bytes 393224 | tf_op jit(solution)/shard_map/ppermute | solution.py:356
  15.3 4.5 %all_gather.3.near_ref = bf16[32,16,256]{2,1,0:T(8,128)(2,1)S(1)} all-gather(bf16[16,16,256]{2,1,0:T(8,128)(2,1)S(1)} %get-tuple-element.15), channel_id=1, replica_groups={{0,16},{32,48},{64,80},{96,112},{128,144},{160,176},{192,208},{224,240}..., dimensions={0}, use_global_device_ids=true | all-gather | bytes 393216 | tf_op jit(solution)/shard_map/all_gather | solution.py:358
  19.8 0.0 collective-permute-done.far_ref
  19.8 0.0 copy-done
  19.8 1.0 %transport.1 = bf16[16,64,256]{2,1,0:T(8,128)(2,1)S(1)} custom-call(s32[6,16]{1,0:T(8,128)S(4)} %get-tuple-element.11.source, s32[6,16]{1,0:T(8,128)S(4)} %get-tuple-element.12.level, bf16[16,64,256]{2,1,0:T(8,128)(2,1)S(1)} %get-tuple-element.13.held, bf16[96,16,256]{2,1,0:T(8,128)(2,1)S(1)} %get-tuple-element.14.rows, ...), custom_call_target="tpu_custom_call" | custom-call | tf_op jit(solution)/shard_map/transport/pallas_call | solution.py:360
  20.8 0.0 copy-start.1
  20.9 0.0 copy-start.2
  20.9 0.0 copy-start.3
  20.9 0.0 copy-start.4
  20.9 26.5 %all_to_all.10.dist_ref = bf16[16,64,256]{2,1,0:T(8,128)(2,1)S(1)} all-to-all(bf16[16,64,256]{2,1,0:T(8,128)(2,1)S(1)} %transport.1), channel_id=1, replica_groups=mesh['space'=32,'vel'=16] {'vel'}, dimensions={0} | all-to-all | bytes 1048576 | tf_op jit(solution)/shard_map/all_to_all | solution.py:381
  47.4 0.0 copy-done.1
  47.4 0.0 copy-done.2
  47.4 0.0 copy-done.3
  47.4 0.0 copy-done.4
  47.4 4.7 %collide.1 = bf16[16,64,256]{2,1,0:T(8,128)(2,1)S(1)} custom-call(bf16[16,64,256]{2,1,0:T(8,128)(2,1)S(1)} %all_to_all.10.dist_ref, f32[4,4096]{1,0:T(4,128)S(1)} %copy-done.4, f32[5,4096]{1,0:T(8,128)S(1)} %copy-done.3, bf16[2,256,256]{2,1,0:T(8,128)(2,1)S(1)} %copy-done.2, bf16[2,256,256]{2,1,0:T(8,128)(2,1)S(1)} %copy-done.1), custom_call_target="tpu_custom_call" | custom-call | tf_op jit(solution)/shard_map/collide/pallas_call | solution.py:382
  52.0 20.0 %all_to_all.11 = bf16[16,64,256]{2,1,0:T(8,128)(2,1)S(1)} all-to-all(bf16[16,64,256]{2,1,0:T(8,128)(2,1)S(1)} %collide.1), channel_id=1, replica_groups=mesh['space'=32,'vel'=16] {'vel'}, dimensions={0} | all-to-all | bytes 1048576 | tf_op jit(solution)/shard_map/all_to_all | solution.py:390
  72.1 0.8 %copy.12 = bf16[16,64,256]{2,1,0:T(8,128)(2,1)} copy(bf16[16,64,256]{2,1,0:T(8,128)(2,1)S(1)} %all_to_all.11) | data formatting | bytes 1048576
Async XLA Ops:
  0.0 19.8 %copy-start = (bf16[33,64,128]{2,1,0:T(8,128)(2,1)S(1)}, bf16[33,64,128]{2,1,0:T(8,128)(2,1)}, u32[]{:S(2)}) copy-start(bf16[33,64,128]{2,1,0:T(8,128)(2,1)} %constant.6.clone.table_ref) | copy-start | bytes 1622020
  1.6 18.2 %collective-permute-start = (bf16[16,16,256]{2,1,0:T(8,128)(2,1)S(1)}, bf16[16,16,256]{2,1,0:T(8,128)(2,1)S(1)}, u32[]{:S(2)}, u32[]{:S(2)}) collective-permute-start(bf16[16,16,256]{2,1,0:T(8,128)(2,1)S(1)} %get-tuple-element.16), channel_id=1, source_target_pairs={{16,32},{32,16},{48,64},{64,48},{80,96},{96,80},{112,128},{128,112... | collective-permute-start | bytes 393224 | tf_op jit(solution)/shard_map/ppermute | solution.py:356
  20.8 26.5 %copy-start.1 = (bf16[2,256,256]{2,1,0:T(8,128)(2,1)S(1)}, bf16[2,256,256]{2,1,0:T(8,128)(2,1)}, u32[]{:S(2)}) copy-start(bf16[2,256,256]{2,1,0:T(8,128)(2,1)} %constant.8.clone.back_ref) | copy-start | bytes 786436
  20.9 26.5 %copy-start.2 = (bf16[2,256,256]{2,1,0:T(8,128)(2,1)S(1)}, bf16[2,256,256]{2,1,0:T(8,128)(2,1)}, u32[]{:S(2)}) copy-start(bf16[2,256,256]{2,1,0:T(8,128)(2,1)} %constant.7.clone.into_ref) | copy-start | bytes 786436
  20.9 26.5 %copy-start.3 = (f32[5,4096]{1,0:T(8,128)S(1)}, f32[5,4096]{1,0:T(8,128)}, u32[]{:S(2)}) copy-start(f32[5,4096]{1,0:T(8,128)} %beta_ref.1) | copy-start | bytes 245764
  20.9 26.5 %copy-start.4 = (f32[4,4096]{1,0:T(4,128)S(1)}, f32[4,4096]{1,0:T(4,128)}, u32[]{:S(2)}) copy-start(f32[4,4096]{1,0:T(4,128)} %alpha_ref.1) | copy-start | bytes 196612

commit v7 on v5

--- a/solution.py
+++ b/solution.py
@@ -10,6 +10,7 @@
 VSIDE = 16
 SLOTS = 16
 GROUP = 16
+AHEAD = 3
 SCOPED = 16 << 20
 
 
@@ -209,23 +210,25 @@
     back_ref,
     ahead_ref,
     held,
-    rows,
     source,
     level,
+    picks,
     faces,
     count,
     sems,
 ):
     pairs = (faces_hbm, faces), (count_hbm, count), (dist_hbm, held), (source_hbm, source)
     copies = fetched(sems, *pairs, (level_hbm, level))
+    picks[...] = face_selector(held.shape[1]).reshape(picks.shape)
     for copy in copies:
         copy.wait()
-    extract_traces(held, rows)
-    rows[6 * held.shape[0]] = jnp.zeros(rows.shape[1:], jnp.bfloat16)
     for way, out in enumerate((back_ref, ahead_ref)):
         for slot in range(SLOTS):
             keep = jnp.where(slot < count[0, way], 1.0, 0.0).astype(jnp.bfloat16)
-            out[slot] = rows[faces[0, way, slot]] * keep
+            number = faces[0, way, slot]
+            element = number // 6
+            trace = dot(picks[number - 6 * element], held[element])
+            out[slot] = trace.astype(jnp.bfloat16) * keep
 
 
 def add_lifts(left, stacked, total):
@@ -237,7 +240,7 @@
     return total
 
 
-def local_kernel(source, level, held, rows, table_ref, out_ref, left_ref, stack):
+def local_kernel(source, level, held, table_ref, out_ref, left_ref, rows, stack):
     elements, nodes, width = held.shape
     faces = 6 * elements
     speeds = local_speeds((1, width))
@@ -250,6 +253,8 @@
         member = jnp.logical_and(on, digits[face // 2] == 3 * (face % 2))
         loss = loss + jnp.where(member, jnp.abs(wide[face // 2]), 0.0)
     keep = 1.0 - courant * lift_weight * loss
+    extract_traces(held, rows)
+    rows[faces] = jnp.zeros((16, width), jnp.bfloat16)
     gradient = table_ref[30:].reshape(3 * nodes, table_ref.shape[2])[:, :nodes]
     for at in range(elements):
         for face in range(6):
@@ -295,30 +300,41 @@
         cube = array.reshape(VSIDE, GROUP, plane)
         return [cube[i] for i in range(VSIDE)]
 
-    for start in range(0, nodes, GROUP):
+    order = [(kern, mode) for mode in range(modes) for kern in (alpha_ref, beta_ref)]
+    order.append((beta_ref, modes))
+
+    def gathered(start, ahead):
         group = slice(start, start + GROUP)
         values = dist_ref[:, group, :].reshape(VSIDE * GROUP, plane)
         spectrum = cosine_forward(planes(dot(values, into_ref[0]) + dot(values, into_ref[1])))
         spectrum[0] = 0.5 * spectrum[0]
-
-        def field(kern, row):
-            parts = [
-                (spectrum[i] * kern[row : row + 1, i * plane : (i + 1) * plane]).astype(jnp.bfloat16)
-                for i in range(VSIDE)
-            ]
-            left = jnp.concatenate(parts, axis=0)
-            return cosine_backward(planes(dot(left, back_ref[0]) + dot(left, back_ref[1])))
-
-        gain = None
-        for mode in range(modes):
-            pairs = zip(field(alpha_ref, mode), field(beta_ref, mode))
-            products = [first * second for first, second in pairs]
-            gain = products if mode == 0 else [a + b for a, b in zip(gain, products)]
-        loss = field(beta_ref, modes)
-        for i in range(VSIDE):
-            value = dist_ref[i, group, :].astype(jnp.float32)
-            total = value + relax_step * (gain[i] - value * loss[i])
-            out_ref[i, group, :] = total.astype(jnp.bfloat16)
+        pending = []
+        for at in range(len(order) + ahead):
+            if at < len(order):
+                kern, row = order[at]
+                parts = [
+                    spectrum[i] * kern[row : row + 1, i * plane : (i + 1) * plane]
+                    for i in range(VSIDE)
+                ]
+                left = jnp.concatenate([part.astype(jnp.bfloat16) for part in parts], axis=0)
+                pending.append(dot(left, back_ref[0]) + dot(left, back_ref[1]))
+            if at >= ahead:
+                yield cosine_backward(planes(pending.pop(0)))
+
+    for start in range(0, nodes, GROUP):
+        group = slice(start, start + GROUP)
+        gain, first = None, None
+        for at, field in enumerate(gathered(start, AHEAD)):
+            if at == 2 * modes:
+                for i in range(VSIDE):
+                    value = dist_ref[i, group, :].astype(jnp.float32)
+                    total = value + relax_step * (gain[i] - value * field[i])
+                    out_ref[i, group, :] = total.astype(jnp.bfloat16)
+            elif at % 2 == 0:
+                first = field
+            else:
+                products = [a * b for a, b in zip(first, field)]
+                gain = products if at == 1 else [a + b for a, b in zip(gain, products)]
 
 
 def in_vmem():
@@ -353,19 +369,19 @@
 
     sources, levels = source_face.T, subface.T
     indices = pltpu.SMEM(sources.shape, jnp.int32)
-    back, ahead, held, rows, source, level = pl.pallas_call(
+    back, ahead, held, source, level = pl.pallas_call(
         send_kernel,
         out_shape=(
             traces,
             traces,
             block,
-            pltpu.VMEM((faces + 1, 16, width), jnp.bfloat16),
             indices,
             indices,
         ),
         in_specs=[in_hbm()] * 5,
-        out_specs=(in_vmem(),) * 4 + (in_smem(),) * 2,
+        out_specs=(in_vmem(),) * 3 + (in_smem(),) * 2,
         scratch_shapes=[
+            pltpu.VMEM((6, 16, nodes), jnp.bfloat16),
             pltpu.SMEM(send_faces.shape, jnp.int32),
             pltpu.SMEM(send_count.shape, jnp.int32),
             pltpu.SemaphoreType.DMA((5,)),
@@ -383,12 +399,15 @@
             pltpu.VMEM(dist.shape, jnp.float32),
             pltpu.VMEM((elements, 3 * nodes, 128), jnp.bfloat16),
         ),
-        in_specs=[in_smem()] * 2 + [in_vmem()] * 3,
+        in_specs=[in_smem()] * 2 + [in_vmem()] * 2,
         out_specs=(in_vmem(), in_vmem()),
-        scratch_shapes=[pltpu.VMEM((elements, 128, width), jnp.bfloat16)],
+        scratch_shapes=[
+            pltpu.VMEM((faces + 1, 16, width), jnp.bfloat16),
+            pltpu.VMEM((elements, 128, width), jnp.bfloat16),
+        ],
         compiler_params=pltpu.CompilerParams(vmem_limit_bytes=SCOPED),
         name="transport_local",
-    )(source, level, *on_chip(held, rows, jnp.asarray(transport_tables())))
+    )(source, level, *on_chip(held, jnp.asarray(transport_tables())))
     updated = pl.pallas_call(
         remote_kernel,
         out_shape=block,

time: 71.7 us -> 71.6 us (level)
  transfers between devices with their start and end apart: 2 -> 2, of which waited for: 2 -> 1; matrix products, arithmetic and copies ran while one was open for 0% -> 0% of each run, Pallas kernels for 1% -> 2%
where the time goes in v7:
time: 71.6 us; the launch traced here: 71.4 us
  blocking collectives  45.9 us (64%)
  starting transfers between devices  15.6 us (22%)
  Pallas kernels  8.18 us (11%)
  local copies, waits for them, and re-layouts  0.82 us (1%)
    all_to_all x1, blocking collectives, on_device(): lax.all_to_all(updated, 'vel', split_axis=0, concat_axis=0, tiled=True)  25.9 us
    all_to_all x1, blocking collectives, on_device(): return lax.all_to_all(mixed, 'vel', split_axis=0, concat_axis=0, tiled=True)  20 us
    ppermute x2, starting transfers between devices, passed_along(): return lax.ppermute(block, axis, route)  15.6 us
    pallas_call x1, Pallas kernels, on_device(): pl.pallas_call(collide_kernel, out_shape=pltpu.VMEM(whole.shape, jnp.bflo...  4.65 us
    pallas_call x1, Pallas kernels, on_device(): pl.pallas_call(send_kernel, out_shape=(traces, traces, block, indices, in...  1.53 us
  transfers between devices with their start and end apart: 2, of which 1 were waited for; matrix products, arithmetic and copies ran while one was open for 0% of the time, Pallas kernels for 2%

profile of v7, /device:TPU:1, one launch (start us, length us, event | category | flops | bytes accessed | tf_op | source)
XLA Modules:
  0.0 71.4 jit_solution(11567169851065209243)
XLA Ops:
  0.0 0.0 copy-start
  0.0 1.5 %send_traces.1 = (bf16[16,16,256]{2,1,0:T(8,128)(2,1)S(1)}, bf16[16,16,256]{2,1,0:T(8,128)(2,1)S(1)}, bf16[16,64,256]{2,1,0:T(8,128)(2,1)S(1)}, s32[6,16]{1,0:T(8,128)S(4)}, s32[6,16]{1,0:T(8,128)S(4)}) custom-call(s32[1,2,16]{2,1,0:T(2,128)} %faces_hbm.1, s32[1,2]{1,0:T(1,128)} %count_hbm.1, s32[6,16]{1,0:T(8,128)} %bitcast.2, s32[6,16]{1,0:T(8,128)} %bitcast.3, ...), custom_call_target="tpu_custom_call" | custom-call | tf_op jit(solution)/shard_map/send_traces/pallas_call | solution.py:372
  1.5 3.9 %collective-permute-start = (bf16[16,16,256]{2,1,0:T(8,128)(2,1)S(1)}, bf16[16,16,256]{2,1,0:T(8,128)(2,1)S(1)}, u32[]{:S(2)}, u32[]{:S(2)}) collective-permute-start(bf16[16,16,256]{2,1,0:T(8,128)(2,1)S(1)} %get-tuple-element.17), channel_id=1, source_target_pairs={{496,0},{0,16},{16,32},{32,48},{48,64},{64,80},{80,96},{96,112},{1... | collective-permute-start | bytes 393224 | tf_op jit(solution)/shard_map/ppermute | solution.py:25
  5.5 11.7 %collective-permute-start.1 = (bf16[16,16,256]{2,1,0:T(8,128)(2,1)S(1)}, bf16[16,16,256]{2,1,0:T(8,128)(2,1)S(1)}, u32[]{:S(2)}, u32[]{:S(2)}) collective-permute-start(bf16[16,16,256]{2,1,0:T(8,128)(2,1)S(1)} %get-tuple-element.18), channel_id=1, source_target_pairs={{16,0},{32,16},{48,32},{64,48},{80,64},{96,80},{112,96},{128,112},... | collective-permute-start | bytes 393224 | tf_op jit(solution)/shard_map/ppermute | solution.py:25
  17.2 0.0 copy-done
  17.2 1.4 %transport_local.1 = (f32[16,64,256]{2,1,0:T(8,128)S(1)}, bf16[16,192,128]{2,1,0:T(8,128)(2,1)S(1)}) custom-call(s32[6,16]{1,0:T(8,128)S(4)} %get-tuple-element.12.source, s32[6,16]{1,0:T(8,128)S(4)} %get-tuple-element.13.level, bf16[16,64,256]{2,1,0:T(8,128)(2,1)S(1)} %get-tuple-element.14.held, bf16[33,64,128]{2,1,0:T(8,128)(2,1)S(1)} %copy-done), custom_call_target="tpu_custom_call" | custom-call | tf_op jit(solution)/shard_map/transport_local/pallas_call | solution.py:396
  18.6 0.0 collective-permute-done.prev_ref
  18.6 0.7 collective-permute-done.1.next_ref
  19.3 0.6 transport_remote.1
  19.9 0.0 copy-start.1
  19.9 0.0 copy-start.2
  19.9 0.0 copy-start.3
  19.9 0.0 copy-start.4
  20.0 25.9 %all_to_all.10.dist_ref = bf16[16,64,256]{2,1,0:T(8,128)(2,1)S(1)} all-to-all(bf16[16,64,256]{2,1,0:T(8,128)(2,1)S(1)} %transport_remote.1), channel_id=1, replica_groups=mesh['space'=32,'vel'=16] {'vel'}, dimensions={0} | all-to-all | bytes 1048576 | tf_op jit(solution)/shard_map/all_to_all | solution.py:429
  45.9 0.0 copy-done.1
  45.9 0.0 copy-done.2
  45.9 0.0 copy-done.3
  45.9 0.0 copy-done.4
  45.9 4.7 %collide.1 = bf16[16,64,256]{2,1,0:T(8,128)(2,1)S(1)} custom-call(bf16[16,64,256]{2,1,0:T(8,128)(2,1)S(1)} %all_to_all.10.dist_ref, f32[4,4096]{1,0:T(4,128)S(1)} %copy-done.4, f32[5,4096]{1,0:T(8,128)S(1)} %copy-done.3, bf16[2,256,256]{2,1,0:T(8,128)(2,1)S(1)} %copy-done.2, bf16[2,256,256]{2,1,0:T(8,128)(2,1)S(1)} %copy-done.1), custom_call_target="tpu_custom_call" | custom-call | tf_op jit(solution)/shard_map/collide/pallas_call | solution.py:430
  50.5 20.0 %all_to_all.11 = bf16[16,64,256]{2,1,0:T(8,128)(2,1)S(1)} all-to-all(bf16[16,64,256]{2,1,0:T(8,128)(2,1)S(1)} %collide.1), channel_id=1, replica_groups=mesh['space'=32,'vel'=16] {'vel'}, dimensions={0} | all-to-all | bytes 1048576 | tf_op jit(solution)/shard_map/all_to_all | solution.py:438
  70.6 0.8 %copy.12 = bf16[16,64,256]{2,1,0:T(8,128)(2,1)} copy(bf16[16,64,256]{2,1,0:T(8,128)(2,1)S(1)} %all_to_all.11) | data formatting | bytes 1048576
Async XLA Ops:
  0.0 17.2 %copy-start = (bf16[33,64,128]{2,1,0:T(8,128)(2,1)S(1)}, bf16[33,64,128]{2,1,0:T(8,128)(2,1)}, u32[]{:S(2)}) copy-start(bf16[33,64,128]{2,1,0:T(8,128)(2,1)} %constant.6.clone.table_ref) | copy-start | bytes 1622020
  1.5 17.1 %collective-permute-start = (bf16[16,16,256]{2,1,0:T(8,128)(2,1)S(1)}, bf16[16,16,256]{2,1,0:T(8,128)(2,1)S(1)}, u32[]{:S(2)}, u32[]{:S(2)}) collective-permute-start(bf16[16,16,256]{2,1,0:T(8,128)(2,1)S(1)} %get-tuple-element.17), channel_id=1, source_target_pairs={{496,0},{0,16},{16,32},{32,48},{48,64},{64,80},{80,96},{96,112},{1... | collective-permute-start | bytes 393224 | tf_op jit(solution)/shard_map/ppermute | solution.py:25
  5.5 13.8 %collective-permute-start.1 = (bf16[16,16,256]{2,1,0:T(8,128)(2,1)S(1)}, bf16[16,16,256]{2,1,0:T(8,128)(2,1)S(1)}, u32[]{:S(2)}, u32[]{:S(2)}) collective-permute-start(bf16[16,16,256]{2,1,0:T(8,128)(2,1)S(1)} %get-tuple-element.18), channel_id=1, source_target_pairs={{16,0},{32,16},{48,32},{64,48},{80,64},{96,80},{112,96},{128,112},... | collective-permute-start | bytes 393224 | tf_op jit(solution)/shard_map/ppermute | solution.py:25
  19.9 26.0 %copy-start.1 = (bf16[2,256,256]{2,1,0:T(8,128)(2,1)S(1)}, bf16[2,256,256]{2,1,0:T(8,128)(2,1)}, u32[]{:S(2)}) copy-start(bf16[2,256,256]{2,1,0:T(8,128)(2,1)} %constant.8.clone.back_ref) | copy-start | bytes 786436
  19.9 25.9 %copy-start.2 = (bf16[2,256,256]{2,1,0:T(8,128)(2,1)S(1)}, bf16[2,256,256]{2,1,0:T(8,128)(2,1)}, u32[]{:S(2)}) copy-start(bf16[2,256,256]{2,1,0:T(8,128)(2,1)} %constant.7.clone.into_ref) | copy-start | bytes 786436
  19.9 25.9 %copy-start.3 = (f32[5,4096]{1,0:T(8,128)S(1)}, f32[5,4096]{1,0:T(8,128)}, u32[]{:S(2)}) copy-start(f32[5,4096]{1,0:T(8,128)} %beta_ref.1) | copy-start | bytes 245764
  19.9 25.9 %copy-start.4 = (f32[4,4096]{1,0:T(4,128)S(1)}, f32[4,4096]{1,0:T(4,128)}, u32[]{:S(2)}) copy-start(f32[4,4096]{1,0:T(4,128)} %alpha_ref.1) | copy-start | bytes 196612

commit v8 on v7

--- a/solution.py
+++ b/solution.py
@@ -217,7 +217,7 @@
     count,
     sems,
 ):
-    pairs = (faces_hbm, faces), (count_hbm, count), (dist_hbm, held), (source_hbm, source)
+    pairs = (dist_hbm, held), (faces_hbm, faces), (count_hbm, count), (source_hbm, source)
     copies = fetched(sems, *pairs, (level_hbm, level))
     picks[...] = face_selector(held.shape[1]).reshape(picks.shape)
     for copy in copies:

time: 71.6 us -> 71.6 us (level)
  no operation moved by 1% of the time
where the time goes in v8:
time: 71.6 us; the launch traced here: 71.4 us
  blocking collectives  45.9 us (64%)
  starting transfers between devices  15.6 us (22%)
  Pallas kernels  8.2 us (11%)
  local copies, waits for them, and re-layouts  0.82 us (1%)
    all_to_all x1, blocking collectives, on_device(): lax.all_to_all(updated, 'vel', split_axis=0, concat_axis=0, tiled=True)  25.9 us
    all_to_all x1, blocking collectives, on_device(): return lax.all_to_all(mixed, 'vel', split_axis=0, concat_axis=0, tiled=True)  20 us
    ppermute x2, starting transfers between devices, passed_along(): return lax.ppermute(block, axis, route)  15.6 us
    pallas_call x1, Pallas kernels, on_device(): pl.pallas_call(collide_kernel, out_shape=pltpu.VMEM(whole.shape, jnp.bflo...  4.65 us
    pallas_call x1, Pallas kernels, on_device(): pl.pallas_call(send_kernel, out_shape=(traces, traces, block, indices, in...  1.54 us
  transfers between devices with their start and end apart: 2, of which 1 were waited for; matrix products, arithmetic and copies ran while one was open for 0% of the time, Pallas kernels for 2%

profile of v8, /device:TPU:1, one launch (start us, length us, event | category | flops | bytes accessed | tf_op | source)
XLA Modules:
  0.0 71.4 jit_solution(5171850907403569502)
XLA Ops:
  0.0 0.0 copy-start
  0.0 1.5 %send_traces.1 = (bf16[16,16,256]{2,1,0:T(8,128)(2,1)S(1)}, bf16[16,16,256]{2,1,0:T(8,128)(2,1)S(1)}, bf16[16,64,256]{2,1,0:T(8,128)(2,1)S(1)}, s32[6,16]{1,0:T(8,128)S(4)}, s32[6,16]{1,0:T(8,128)S(4)}) custom-call(s32[1,2,16]{2,1,0:T(2,128)} %faces_hbm.1, s32[1,2]{1,0:T(1,128)} %count_hbm.1, s32[6,16]{1,0:T(8,128)} %bitcast.2, s32[6,16]{1,0:T(8,128)} %bitcast.3, ...), custom_call_target="tpu_custom_call" | custom-call | tf_op jit(solution)/shard_map/send_traces/pallas_call | solution.py:372
  1.6 3.9 %collective-permute-start = (bf16[16,16,256]{2,1,0:T(8,128)(2,1)S(1)}, bf16[16,16,256]{2,1,0:T(8,128)(2,1)S(1)}, u32[]{:S(2)}, u32[]{:S(2)}) collective-permute-start(bf16[16,16,256]{2,1,0:T(8,128)(2,1)S(1)} %get-tuple-element.17), channel_id=1, source_target_pairs={{496,0},{0,16},{16,32},{32,48},{48,64},{64,80},{80,96},{96,112},{1... | collective-permute-start | bytes 393224 | tf_op jit(solution)/shard_map/ppermute | solution.py:25
  5.5 11.7 %collective-permute-start.1 = (bf16[16,16,256]{2,1,0:T(8,128)(2,1)S(1)}, bf16[16,16,256]{2,1,0:T(8,128)(2,1)S(1)}, u32[]{:S(2)}, u32[]{:S(2)}) collective-permute-start(bf16[16,16,256]{2,1,0:T(8,128)(2,1)S(1)} %get-tuple-element.18), channel_id=1, source_target_pairs={{16,0},{32,16},{48,32},{64,48},{80,64},{96,80},{112,96},{128,112},... | collective-permute-start | bytes 393224 | tf_op jit(solution)/shard_map/ppermute | solution.py:25
  17.2 0.0 copy-done
  17.2 1.4 %transport_local.1 = (f32[16,64,256]{2,1,0:T(8,128)S(1)}, bf16[16,192,128]{2,1,0:T(8,128)(2,1)S(1)}) custom-call(s32[6,16]{1,0:T(8,128)S(4)} %get-tuple-element.12.source, s32[6,16]{1,0:T(8,128)S(4)} %get-tuple-element.13.level, bf16[16,64,256]{2,1,0:T(8,128)(2,1)S(1)} %get-tuple-element.14.held, bf16[33,64,128]{2,1,0:T(8,128)(2,1)S(1)} %copy-done), custom_call_target="tpu_custom_call" | custom-call | tf_op jit(solution)/shard_map/transport_local/pallas_call | solution.py:396
  18.6 0.0 collective-permute-done.prev_ref
  18.6 0.7 collective-permute-done.1.next_ref
  19.3 0.6 transport_remote.1
  19.9 0.0 copy-start.1
  19.9 0.0 copy-start.2
  20.0 0.0 copy-start.3
  20.0 0.0 copy-start.4
  20.0 25.9 %all_to_all.10.dist_ref = bf16[16,64,256]{2,1,0:T(8,128)(2,1)S(1)} all-to-all(bf16[16,64,256]{2,1,0:T(8,128)(2,1)S(1)} %transport_remote.1), channel_id=1, replica_groups=mesh['space'=32,'vel'=16] {'vel'}, dimensions={0} | all-to-all | bytes 1048576 | tf_op jit(solution)/shard_map/all_to_all | solution.py:429
  45.9 0.0 copy-done.1
  45.9 0.0 copy-done.2
  45.9 0.0 copy-done.3
  45.9 0.0 copy-done.4
  45.9 4.7 %collide.1 = bf16[16,64,256]{2,1,0:T(8,128)(2,1)S(1)} custom-call(bf16[16,64,256]{2,1,0:T(8,128)(2,1)S(1)} %all_to_all.10.dist_ref, f32[4,4096]{1,0:T(4,128)S(1)} %copy-done.4, f32[5,4096]{1,0:T(8,128)S(1)} %copy-done.3, bf16[2,256,256]{2,1,0:T(8,128)(2,1)S(1)} %copy-done.2, bf16[2,256,256]{2,1,0:T(8,128)(2,1)S(1)} %copy-done.1), custom_call_target="tpu_custom_call" | custom-call | tf_op jit(solution)/shard_map/collide/pallas_call | solution.py:430
  50.6 20.0 %all_to_all.11 = bf16[16,64,256]{2,1,0:T(8,128)(2,1)S(1)} all-to-all(bf16[16,64,256]{2,1,0:T(8,128)(2,1)S(1)} %collide.1), channel_id=1, replica_groups=mesh['space'=32,'vel'=16] {'vel'}, dimensions={0} | all-to-all | bytes 1048576 | tf_op jit(solution)/shard_map/all_to_all | solution.py:438
  70.6 0.8 %copy.12 = bf16[16,64,256]{2,1,0:T(8,128)(2,1)} copy(bf16[16,64,256]{2,1,0:T(8,128)(2,1)S(1)} %all_to_all.11) | data formatting | bytes 1048576
Async XLA Ops:
  0.0 17.2 %copy-start = (bf16[33,64,128]{2,1,0:T(8,128)(2,1)S(1)}, bf16[33,64,128]{2,1,0:T(8,128)(2,1)}, u32[]{:S(2)}) copy-start(bf16[33,64,128]{2,1,0:T(8,128)(2,1)} %constant.6.clone.table_ref) | copy-start | bytes 1622020
  1.6 17.1 %collective-permute-start = (bf16[16,16,256]{2,1,0:T(8,128)(2,1)S(1)}, bf16[16,16,256]{2,1,0:T(8,128)(2,1)S(1)}, u32[]{:S(2)}, u32[]{:S(2)}) collective-permute-start(bf16[16,16,256]{2,1,0:T(8,128)(2,1)S(1)} %get-tuple-element.17), channel_id=1, source_target_pairs={{496,0},{0,16},{16,32},{32,48},{48,64},{64,80},{80,96},{96,112},{1... | collective-permute-start | bytes 393224 | tf_op jit(solution)/shard_map/ppermute | solution.py:25
  5.5 13.8 %collective-permute-start.1 = (bf16[16,16,256]{2,1,0:T(8,128)(2,1)S(1)}, bf16[16,16,256]{2,1,0:T(8,128)(2,1)S(1)}, u32[]{:S(2)}, u32[]{:S(2)}) collective-permute-start(bf16[16,16,256]{2,1,0:T(8,128)(2,1)S(1)} %get-tuple-element.18), channel_id=1, source_target_pairs={{16,0},{32,16},{48,32},{64,48},{80,64},{96,80},{112,96},{128,112},... | collective-permute-start | bytes 393224 | tf_op jit(solution)/shard_map/ppermute | solution.py:25
  19.9 26.0 %copy-start.1 = (bf16[2,256,256]{2,1,0:T(8,128)(2,1)S(1)}, bf16[2,256,256]{2,1,0:T(8,128)(2,1)}, u32[]{:S(2)}) copy-start(bf16[2,256,256]{2,1,0:T(8,128)(2,1)} %constant.8.clone.back_ref) | copy-start | bytes 786436
  19.9 25.9 %copy-start.2 = (bf16[2,256,256]{2,1,0:T(8,128)(2,1)S(1)}, bf16[2,256,256]{2,1,0:T(8,128)(2,1)}, u32[]{:S(2)}) copy-start(bf16[2,256,256]{2,1,0:T(8,128)(2,1)} %constant.7.clone.into_ref) | copy-start | bytes 786436
  20.0 25.9 %copy-start.3 = (f32[5,4096]{1,0:T(8,128)S(1)}, f32[5,4096]{1,0:T(8,128)}, u32[]{:S(2)}) copy-start(f32[5,4096]{1,0:T(8,128)} %beta_ref.1) | copy-start | bytes 245764
  20.0 25.9 %copy-start.4 = (f32[4,4096]{1,0:T(4,128)S(1)}, f32[4,4096]{1,0:T(4,128)}, u32[]{:S(2)}) copy-start(f32[4,4096]{1,0:T(4,128)} %alpha_ref.1) | copy-start | bytes 196612
